TPU v7x, 128 devices: a whole 4x4x4 slice. The times are simulated.
128 devices in a mesh: lat: 8 (over x_lo, z), lon: 16 (over x_hi, y, core).
Axes of the slice: x: 4 (x_hi: 2, x_lo: 2; x = x_hi * 2 + x_lo), y: 4, z: 4, core: 2. Of those that a mesh axis runs over, the one named last changes fastest.
Arguments:
- features: bfloat16 [32, 1024, 2048], P(None, 'lat', 'lon'), may hold values from -6 to 6
- cotangent: bfloat16 [32, 1024, 2048], P(None, 'lat', 'lon'), may hold values from -6 to 6
- sea_mask: int32 [1024, 2048], P('lat', 'lon'), may hold values 0 or 1
- weights: bfloat16 [5, 32, 32], replicated, may hold values from -1 to 1
Outputs:
- feature_grad: bfloat16 [32, 1024, 2048], P(None, 'lat', 'lon')
- weight_grad: float32 [5, 32, 32], replicated
Inputs may be any that keep to these rules, and one draw needn't show every extreme that they name: `sea_mask`: 1 marks a sea cell, 0 a land cell.
All inputs are finite; a program needn't handle non-finite values. No bound on the sum of `sea_mask` on one device may be relied on, other than what follows from the above.
Results may differ from a plain program's by a relative error of at most 0.0069.
Values sent between devices are 32-bit elements; how exact they have to be, the bound alone decides.
A program may use at most 128 MiB of HBM per device.

v0:
```python
import math

import jax
import jax.numpy as jnp
from jax import lax
from jax.sharding import PartitionSpec as P

K = 4


NEIGHBOURS = ((0, -1), (0, 1), (-1, 0), (1, 0), (-1, 1), (1, -1))


def padded_2(cells, sides, width, closed):
    for axis, dim in sides:
        count = lax.axis_size(axis)
        ends = count if closed else count - 1
        head = lax.slice_in_dim(cells, 0, width, axis=dim)
        tail = lax.slice_in_dim(cells, cells.shape[dim] - width, cells.shape[dim], axis=dim)
        cells = jnp.concatenate(
            [
                lax.ppermute(tail, axis, [(i, (i + 1) % count) for i in range(ends)]),
                cells,
                lax.ppermute(head, axis, [((i + 1) % count, i) for i in range(ends)]),
            ],
            axis=dim,
        )
    return cells


def neigh_sum(padded, outer_pad, inner_pad):
    row_count = padded.shape[-2] - 2 * (outer_pad - inner_pad)
    col_count = padded.shape[-1] - 2 * (outer_pad - inner_pad)
    base = outer_pad - inner_pad
    summed = None
    for step_row, step_col in NEIGHBOURS:
        shifted = padded[
            ...,
            base + step_row : base + step_row + row_count,
            base + step_col : base + step_col + col_count,
        ]
        summed = shifted if summed is None else summed + shifted
    return summed


def extend(cells_in, depth_cells):
    widened = padded_2(cells_in, (("lon", 2),), depth_cells, True)
    return padded_2(widened, (("lat", 1),), depth_cells, False)


def extend_flags(flag_cells, depth_cells):
    widened = padded_2(flag_cells, (("lon", 1),), depth_cells, True)
    return padded_2(widened, (("lat", 0),), depth_cells, False)


def local(features, cotangent, sea_mask, weights):
    flags_three = extend_flags(sea_mask, 3).astype(jnp.float32)
    degree = neigh_sum(flags_three, 3, 2)
    scale_two = flags_three[1:-1, 1:-1] / jnp.sqrt(jnp.maximum(degree, 1.0))
    scale_one = scale_two[1:-1, 1:-1]
    scale_zero = scale_two[2:-2, 2:-2]
    sea_cells = sea_mask.astype(jnp.float32)

    def laplace(cells_in):
        padded = extend(cells_in, 1)
        return -scale_zero * neigh_sum(scale_one * padded, 1, 0)

    initial = sea_cells * features.astype(jnp.float32)

    def keep_visit(carried, term):
        return carried + (term.astype(jnp.bfloat16),)

    carried = ()
    carried = keep_visit(carried, initial)
    previous = initial
    current = laplace(initial)
    carried = keep_visit(carried, current)
    for order_k in range(2, K + 1):
        advanced = 2.0 * laplace(current) - previous
        carried = keep_visit(carried, advanced)
        previous, current = (current, advanced)
    mixed = jnp.zeros(features.shape, jnp.float32)
    for index_k in range(K + 1):
        mixed = mixed + jnp.einsum(
            "cd,cij->dij", weights[index_k], carried[index_k], preferred_element_type=jnp.float32
        )
    activated = jnp.tanh(mixed)
    grad_mix = (cotangent.astype(jnp.float32) * (1.0 - activated * activated)).astype(jnp.bfloat16)
    weight_terms = jnp.stack(
        [
            jnp.einsum("cij,dij->cd", kept, grad_mix, preferred_element_type=jnp.float32)
            for kept in carried
        ]
    )
    summed = lax.psum(weight_terms, ("lat", "lon"))
    grid_cells = features.shape[1] * lax.axis_size("lat") * features.shape[2] * lax.axis_size("lon")
    weight_grad = summed * (1.0 / math.sqrt(grid_cells))

    def project(index_k):
        return jnp.einsum(
            "cd,dij->cij", weights[index_k], grad_mix, preferred_element_type=jnp.float32
        )

    upper_one = project(K)
    upper_two = jnp.zeros(features.shape, jnp.float32)
    for index_k in range(K - 1, 0, -1):
        fresh = project(index_k) + 2.0 * laplace(upper_one) - upper_two
        upper_two, upper_one = (upper_one, fresh)
    result = project(0) + laplace(upper_one) - upper_two
    feature_grad = (sea_cells * result).astype(jnp.bfloat16)
    return (feature_grad, weight_grad)


def solution(mesh):
    placed = (P(None, "lat", "lon"), P(None, "lat", "lon"), P("lat", "lon"), P())
    return jax.shard_map(
        local, mesh=mesh, in_specs=placed, out_specs=(P(None, "lat", "lon"), P()), check_vma=False
    )
```

profile of v0, /device:TPU:96, one launch (start us, length us, event | category | flops | bytes accessed | tf_op | source)
XLA Modules:
  0.0 408.1 jit_solution(406099193958542431)
XLA Ops:
  1.7 5.3 %collective-permute-start.1 = (s32[128,3]{1,0:T(8,128)S(1)}, s32[128,3]{1,0:T(8,128)S(1)}, u32[]{:S(2)}, u32[]{:S(2)}) collective-permute-start(s32[128,3]{1,0:T(8,128)S(1)} %get-tuple-element.41), channel_id=1, source_target_pairs={{1,0},{2,1},{3,2},{4,3},{5,4},{6,5},{7,6},{8,7},{9,8},{10,9},{11,1... | collective-permute-start | bytes 4616 | tf_op jit(solution)/shard_map/ppermute | solution.py:24
  12.0 3.8 collective-permute-start.3
  24.0 5.4 %collective-permute-start.5 = (f32[32,128,1]{1,0,2:T(8,128)S(1)}, f32[32,128,1]{1,0,2:T(8,128)S(1)}, u32[]{:S(2)}, u32[]{:S(2)}) collective-permute-start(f32[32,128,1]{1,0,2:T(8,128)S(1)} %copy.23), channel_id=1, source_target_pairs={{1,0},{2,1},{3,2},{4,3},{5,4},{6,5},{7,6},{8,7},{9,8},{10,9},{11,1... | collective-permute-start | bytes 49160 | tf_op jit(solution)/shard_map/ppermute | solution.py:24
  29.8 2.9 copy.24
  32.7 2.8 copy.25
  36.5 4.3 %collective-permute-start.6 = (f32[32,1,130]{2,0,1:T(8,128)S(1)}, f32[32,1,130]{2,0,1:T(8,128)S(1)}, u32[]{:S(2)}, u32[]{:S(2)}) collective-permute-start(f32[32,1,130]{2,0,1:T(8,128)S(1)} %get-tuple-element.20), channel_id=1, source_target_pairs={{0,16},{16,32},{32,48},{48,64},{64,80},{80,96},{96,112},{1,17},{17... | collective-permute-start | bytes 49928 | tf_op jit(solution)/shard_map/ppermute | solution.py:22
  43.5 5.3 %collective-permute-done.7 = f32[32,1,130]{2,0,1:T(8,128)S(1)} collective-permute-done((f32[32,1,130]{2,0,1:T(8,128)S(1)}, f32[32,1,130]{2,0,1:T(8,128)S(1)}, u32[]{:S(2)}, u32[]{:S(2)}) %collective-permute-start.7) | collective-permute-done | bytes 16672 | tf_op jit(solution)/shard_map/ppermute | solution.py:24
  61.6 5.4 %collective-permute-start.9 = (f32[32,128,1]{1,0,2:T(8,128)S(1)}, f32[32,128,1]{1,0,2:T(8,128)S(1)}, u32[]{:S(2)}, u32[]{:S(2)}) collective-permute-start(f32[32,128,1]{1,0,2:T(8,128)S(1)} %copy.28), channel_id=1, source_target_pairs={{1,0},{2,1},{3,2},{4,3},{5,4},{6,5},{7,6},{8,7},{9,8},{10,9},{11,1... | collective-permute-start | bytes 49160 | tf_op jit(solution)/shard_map/ppermute | solution.py:24
  67.0 2.9 copy.29
  69.9 2.9 copy.30
  75.9 4.2 %collective-permute-start.11 = (f32[32,1,130]{2,0,1:T(8,128)S(1)}, f32[32,1,130]{2,0,1:T(8,128)S(1)}, u32[]{:S(2)}, u32[]{:S(2)}) collective-permute-start(f32[32,1,130]{2,0,1:T(8,128)S(1)} %get-tuple-element.19), channel_id=1, source_target_pairs={{16,0},{32,16},{48,32},{64,48},{80,64},{96,80},{112,96},{17,1},{33... | collective-permute-start | bytes 49928 | tf_op jit(solution)/shard_map/ppermute | solution.py:24
  80.1 3.8 collective-permute-done.11
  86.4 4.1 %fusion.25 = f32[32,128,128]{2,0,1:T(8,128)S(1)} fusion(f32[32,130,130]{2,0,1:T(8,128)S(1)} %maximum_multiply_fusion.1, f32[128,128]{1,0:T(8,128)S(1)} %slice_negate_fusion, bf16[32,128,128]{2,1,0:T(8,128)(2,1)S(1)} %copy-done.33, f32[128,128]{1,0:T(8,128)S(1)} %convert_element_type.33), kind=kLoop, calls=%fused_computation.64 | loop fusion | flops 5242880 | bytes 15859712 | tf_op jit(solution)/shard_map/sub | solution.py:79
  98.7 5.4 %collective-permute-start.13 = (f32[32,128,1]{1,0,2:T(8,128)S(1)}, f32[32,128,1]{1,0,2:T(8,128)S(1)}, u32[]{:S(2)}, u32[]{:S(2)}) collective-permute-start(f32[32,128,1]{1,0,2:T(8,128)S(1)} %copy.33), channel_id=1, source_target_pairs={{1,0},{2,1},{3,2},{4,3},{5,4},{6,5},{7,6},{8,7},{9,8},{10,9},{11,1... | collective-permute-start | bytes 49160 | tf_op jit(solution)/shard_map/ppermute | solution.py:24
  106.2 2.9 copy.34
  109.1 2.9 copy.35
  115.0 4.4 %collective-permute-start.15 = (f32[32,1,130]{2,0,1:T(8,128)S(1)}, f32[32,1,130]{2,0,1:T(8,128)S(1)}, u32[]{:S(2)}, u32[]{:S(2)}) collective-permute-start(f32[32,1,130]{2,0,1:T(8,128)S(1)} %get-tuple-element.17), channel_id=1, source_target_pairs={{16,0},{32,16},{48,32},{64,48},{80,64},{96,80},{112,96},{17,1},{33... | collective-permute-start | bytes 49928 | tf_op jit(solution)/shard_map/ppermute | solution.py:24
  123.1 3.9 maximum_multiply_fusion.2
  127.0 11.8 %fusion.22 = f32[32,128,128]{2,0,1:T(8,128)S(1)} fusion(f32[32,130,130]{2,0,1:T(8,128)} %maximum_multiply_fusion.2, f32[128,128]{1,0:T(8,128)S(1)} %slice_negate_fusion, f32[32,130,130]{2,0,1:T(8,128)S(1)} %bitcast.102), kind=kLoop, calls=%fused_computation.56 | loop fusion | flops 7340032 | bytes 27328512 | tf_op jit(solution)/shard_map/sub | solution.py:79
  138.8 2.8 fusion.72
  147.0 5.4 %collective-permute-start.17 = (f32[32,128,1]{1,0,2:T(8,128)S(1)}, f32[32,128,1]{1,0,2:T(8,128)S(1)}, u32[]{:S(2)}, u32[]{:S(2)}) collective-permute-start(f32[32,128,1]{1,0,2:T(8,128)S(1)} %copy.38), channel_id=1, source_target_pairs={{1,0},{2,1},{3,2},{4,3},{5,4},{6,5},{7,6},{8,7},{9,8},{10,9},{11,1... | collective-permute-start | bytes 49160 | tf_op jit(solution)/shard_map/ppermute | solution.py:24
  154.2 2.9 copy.39
  157.1 2.8 copy.40
  163.1 4.4 %collective-permute-start.19 = (f32[32,1,130]{2,0,1:T(8,128)S(1)}, f32[32,1,130]{2,0,1:T(8,128)S(1)}, u32[]{:S(2)}, u32[]{:S(2)}) collective-permute-start(f32[32,1,130]{2,0,1:T(8,128)S(1)} %get-tuple-element.15), channel_id=1, source_target_pairs={{16,0},{32,16},{48,32},{64,48},{80,64},{96,80},{112,96},{17,1},{33... | collective-permute-start | bytes 49928 | tf_op jit(solution)/shard_map/ppermute | solution.py:24
  171.3 3.8 maximum_multiply_fusion.3
  175.2 10.2 %fusion.19 = bf16[32,128,128]{2,0,1:T(8,128)(2,1)S(1)} fusion(f32[32,128,128]{2,0,1:T(8,128)S(1)} %fusion.25, f32[32,130,130]{2,0,1:T(8,128)} %maximum_multiply_fusion.3, f32[128,128]{1,0:T(8,128)S(1)} %slice_negate_fusion), kind=kLoop, calls=%fused_computation.48 | loop fusion | flops 4718592 | bytes 15794176 | tf_op jit(solution)/shard_map/convert_element_type | solution.py:71
  185.4 5.6 %fusion.27 = bf16[32,128,128]{2,0,1:T(8,128)(2,1)S(1)} fusion(f32[128,128,32]{1,2,0:T(8,128)} %fusion.34, f32[128,128,32]{1,2,0:T(8,128)} %fusion.37, f32[128,128,32]{1,2,0:T(8,128)} %fusion.43, f32[128,128,32]{1,2,0:T(8,128)} %fusion.40, bf16[32,128,128]{2,0,1:T(8,128)(2,1)S(1)} %fusion.19, bf16[32,128,128]{2,1,0:T(8,128)(2,1)} %param.5, ...), kind=kOutput, calls=%fused_computation.76 | convolution fusion | flops 38273024 | bytes 11542528 | tf_op jit(solution)/shard_map/cd,cij->dij/dot_general | solution.py:84
  191.4 2.9 fusion.71
  199.7 5.4 %collective-permute-start.21 = (f32[32,128,1]{1,0,2:T(8,128)S(1)}, f32[32,128,1]{1,0,2:T(8,128)S(1)}, u32[]{:S(2)}, u32[]{:S(2)}) collective-permute-start(f32[32,128,1]{1,0,2:T(8,128)S(1)} %copy.48), channel_id=1, source_target_pairs={{1,0},{2,1},{3,2},{4,3},{5,4},{6,5},{7,6},{8,7},{9,8},{10,9},{11,1... | collective-permute-start | bytes 49160 | tf_op jit(solution)/shard_map/ppermute | solution.py:24
  205.0 2.9 copy.49
  208.0 2.9 copy.50
  214.5 3.7 collective-permute-start.23
  218.2 4.2 %collective-permute-done.23 = f32[32,1,130]{2,0,1:T(8,128)S(1)} collective-permute-done((f32[32,1,130]{2,0,1:T(8,128)S(1)}, f32[32,1,130]{2,0,1:T(8,128)S(1)}, u32[]{:S(2)}, u32[]{:S(2)}) %collective-permute-start.23) | collective-permute-done | bytes 16672 | tf_op jit(solution)/shard_map/ppermute | solution.py:24
  235.3 5.4 %collective-permute-start.25 = (f32[32,128,1]{1,0,2:T(8,128)S(1)}, f32[32,128,1]{1,0,2:T(8,128)S(1)}, u32[]{:S(2)}, u32[]{:S(2)}) collective-permute-start(f32[32,128,1]{1,0,2:T(8,128)S(1)} %copy.52), channel_id=1, source_target_pairs={{1,0},{2,1},{3,2},{4,3},{5,4},{6,5},{7,6},{8,7},{9,8},{10,9},{11,1... | collective-permute-start | bytes 49160 | tf_op jit(solution)/shard_map/ppermute | solution.py:24
  243.5 2.9 copy.53
  246.4 2.9 copy.54
  252.5 4.1 %collective-permute-start.27 = (f32[32,1,130]{2,0,1:T(8,128)S(1)}, f32[32,1,130]{2,0,1:T(8,128)S(1)}, u32[]{:S(2)}, u32[]{:S(2)}) collective-permute-start(f32[32,1,130]{2,0,1:T(8,128)S(1)} %get-tuple-element.11), channel_id=1, source_target_pairs={{16,0},{32,16},{48,32},{64,48},{80,64},{96,80},{112,96},{17,1},{33... | collective-permute-start | bytes 49928 | tf_op jit(solution)/shard_map/ppermute | solution.py:24
  273.4 5.4 %collective-permute-start.29 = (f32[32,128,1]{1,0,2:T(8,128)S(1)}, f32[32,128,1]{1,0,2:T(8,128)S(1)}, u32[]{:S(2)}, u32[]{:S(2)}) collective-permute-start(f32[32,128,1]{1,0,2:T(8,128)S(1)} %copy.56), channel_id=1, source_target_pairs={{1,0},{2,1},{3,2},{4,3},{5,4},{6,5},{7,6},{8,7},{9,8},{10,9},{11,1... | collective-permute-start | bytes 49160 | tf_op jit(solution)/shard_map/ppermute | solution.py:24
  279.8 2.9 copy.57
  282.7 2.9 copy.58
  288.7 4.2 %collective-permute-start.31 = (f32[32,1,130]{2,0,1:T(8,128)S(1)}, f32[32,1,130]{2,0,1:T(8,128)S(1)}, u32[]{:S(2)}, u32[]{:S(2)}) collective-permute-start(f32[32,1,130]{2,0,1:T(8,128)S(1)} %get-tuple-element.9), channel_id=1, source_target_pairs={{16,0},{32,16},{48,32},{64,48},{80,64},{96,80},{112,96},{17,1},{33... | collective-permute-start | bytes 49928 | tf_op jit(solution)/shard_map/ppermute | solution.py:24
  306.9 3.2 copy.60
  310.2 5.3 %collective-permute-start.33 = (f32[32,128,1]{1,0,2:T(8,128)}, f32[32,128,1]{1,0,2:T(8,128)}, u32[]{:S(2)}, u32[]{:S(2)}) collective-permute-start(f32[32,128,1]{1,0,2:T(8,128)} %copy.60), channel_id=1, source_target_pairs={{1,0},{2,1},{3,2},{4,3},{5,4},{6,5},{7,6},{8,7},{9,8},{10,9},{11,1... | collective-permute-start | bytes 49160 | tf_op jit(solution)/shard_map/ppermute | solution.py:24
  317.8 62.9 %psum.7 = f32[5,32,32]{2,1,0:T(8,128)S(1)} all-reduce(f32[5,32,32]{2,1,0:T(8,128)} %fusion.28), channel_id=1, replica_groups=mesh['lat'=8,'lon'=16] {'lat','lon'}, use_global_device_ids=true, to_apply=%region_0.0 | all-reduce | flops 5120 | bytes 40960 | tf_op jit(solution)/shard_map/psum | solution.py:95
  380.7 3.6 copy.61
  384.3 3.6 copy.62
  388.9 4.4 %collective-permute-start.34 = (f32[32,1,130]{2,0,1:T(8,128)S(1)}, f32[32,1,130]{2,0,1:T(8,128)S(1)}, u32[]{:S(2)}, u32[]{:S(2)}) collective-permute-start(f32[32,1,130]{2,0,1:T(8,128)S(1)} %get-tuple-element.6), channel_id=1, source_target_pairs={{0,16},{16,32},{32,48},{48,64},{64,80},{80,96},{96,112},{1,17},{17... | collective-permute-start | bytes 49928 | tf_op jit(solution)/shard_map/ppermute | solution.py:22
  396.2 5.0 %collective-permute-done.35 = f32[32,1,130]{2,0,1:T(8,128)S(1)} collective-permute-done((f32[32,1,130]{2,0,1:T(8,128)S(1)}, f32[32,1,130]{2,0,1:T(8,128)S(1)}, u32[]{:S(2)}, u32[]{:S(2)}) %collective-permute-start.35) | collective-permute-done | bytes 16672 | tf_op jit(solution)/shard_map/ppermute | solution.py:24
  (189 shorter events, 143.2 us)
Async XLA Ops:
  1.7 8.2 %collective-permute-start = (s32[128,3]{1,0:T(8,128)S(1)}, s32[128,3]{1,0:T(8,128)S(1)}, u32[]{:S(2)}, u32[]{:S(2)}) collective-permute-start(s32[128,3]{1,0:T(8,128)S(1)} %get-tuple-element.40), channel_id=1, source_target_pairs={{0,1},{1,2},{2,3},{3,4},{4,5},{5,6},{6,7},{7,8},{8,9},{9,10},{10,1... | collective-permute-start | bytes 4616 | tf_op jit(solution)/shard_map/ppermute | solution.py:22
  1.7 8.2 %collective-permute-start.1 = (s32[128,3]{1,0:T(8,128)S(1)}, s32[128,3]{1,0:T(8,128)S(1)}, u32[]{:S(2)}, u32[]{:S(2)}) collective-permute-start(s32[128,3]{1,0:T(8,128)S(1)} %get-tuple-element.41), channel_id=1, source_target_pairs={{1,0},{2,1},{3,2},{4,3},{5,4},{6,5},{7,6},{8,7},{9,8},{10,9},{11,1... | collective-permute-start | bytes 4616 | tf_op jit(solution)/shard_map/ppermute | solution.py:24
  10.0 19.4 %collective-permute-start.2 = (s32[3,134]{1,0:T(4,128)S(1)}, s32[3,134]{1,0:T(4,128)S(1)}, u32[]{:S(2)}, u32[]{:S(2)}) collective-permute-start(s32[3,134]{1,0:T(4,128)S(1)} %get-tuple-element.38), channel_id=1, source_target_pairs={{0,16},{16,32},{32,48},{48,64},{64,80},{80,96},{96,112},{1,17},{17... | collective-permute-start | bytes 4832 | tf_op jit(solution)/shard_map/ppermute | solution.py:22
  12.0 17.3 %collective-permute-start.3 = (s32[3,134]{1,0:T(4,128)S(1)}, s32[3,134]{1,0:T(4,128)S(1)}, u32[]{:S(2)}, u32[]{:S(2)}) collective-permute-start(s32[3,134]{1,0:T(4,128)S(1)} %get-tuple-element.39), channel_id=1, source_target_pairs={{16,0},{32,16},{48,32},{64,48},{80,64},{96,80},{112,96},{17,1},{33... | collective-permute-start | bytes 4832 | tf_op jit(solution)/shard_map/ppermute | solution.py:24
  21.3 8.5 %collective-permute-start.4 = (f32[32,128,1]{1,0,2:T(8,128)S(1)}, f32[32,128,1]{1,0,2:T(8,128)S(1)}, u32[]{:S(2)}, u32[]{:S(2)}) collective-permute-start(f32[32,128,1]{1,0,2:T(8,128)S(1)} %copy.22), channel_id=1, source_target_pairs={{0,1},{1,2},{2,3},{3,4},{4,5},{5,6},{6,7},{7,8},{8,9},{9,10},{10,1... | collective-permute-start | bytes 49160 | tf_op jit(solution)/shard_map/ppermute | solution.py:22
  24.0 8.7 %collective-permute-start.5 = (f32[32,128,1]{1,0,2:T(8,128)S(1)}, f32[32,128,1]{1,0,2:T(8,128)S(1)}, u32[]{:S(2)}, u32[]{:S(2)}) collective-permute-start(f32[32,128,1]{1,0,2:T(8,128)S(1)} %copy.23), channel_id=1, source_target_pairs={{1,0},{2,1},{3,2},{4,3},{5,4},{6,5},{7,6},{8,7},{9,8},{10,9},{11,1... | collective-permute-start | bytes 49160 | tf_op jit(solution)/shard_map/ppermute | solution.py:24
  35.5 13.2 %copy-start.17 = (f32[32,128,1]{2,0,1:T(8,128)S(1)}, f32[32,128,1]{2,0,1:T(8,128)}, u32[]{:S(2)}) copy-start(f32[32,128,1]{2,0,1:T(8,128)} %copy.24) | copy-start | bytes 49156
  35.5 13.2 %copy-start.25 = (f32[32,128,1]{2,0,1:T(8,128)S(1)}, f32[32,128,1]{2,0,1:T(8,128)}, u32[]{:S(2)}) copy-start(f32[32,128,1]{2,0,1:T(8,128)} %copy.25) | copy-start | bytes 49156
  36.5 6.9 %collective-permute-start.6 = (f32[32,1,130]{2,0,1:T(8,128)S(1)}, f32[32,1,130]{2,0,1:T(8,128)S(1)}, u32[]{:S(2)}, u32[]{:S(2)}) collective-permute-start(f32[32,1,130]{2,0,1:T(8,128)S(1)} %get-tuple-element.20), channel_id=1, source_target_pairs={{0,16},{16,32},{32,48},{48,64},{64,80},{80,96},{96,112},{1,17},{17... | collective-permute-start | bytes 49928 | tf_op jit(solution)/shard_map/ppermute | solution.py:22
  40.8 7.9 %collective-permute-start.7 = (f32[32,1,130]{2,0,1:T(8,128)S(1)}, f32[32,1,130]{2,0,1:T(8,128)S(1)}, u32[]{:S(2)}, u32[]{:S(2)}) collective-permute-start(f32[32,1,130]{2,0,1:T(8,128)S(1)} %get-tuple-element.21), channel_id=1, source_target_pairs={{16,0},{32,16},{48,32},{64,48},{80,64},{96,80},{112,96},{17,1},{33... | collective-permute-start | bytes 49928 | tf_op jit(solution)/shard_map/ppermute | solution.py:24
  53.5 30.4 %copy-start.1 = (f32[32,128,128]{2,0,1:T(8,128)}, f32[32,128,128]{2,0,1:T(8,128)S(1)}, u32[]{:S(2)}) copy-start(f32[32,128,128]{2,0,1:T(8,128)S(1)} %fusion.26) | copy-start | bytes 6291460
  58.9 8.1 %collective-permute-start.8 = (f32[32,128,1]{1,0,2:T(8,128)S(1)}, f32[32,128,1]{1,0,2:T(8,128)S(1)}, u32[]{:S(2)}, u32[]{:S(2)}) collective-permute-start(f32[32,128,1]{1,0,2:T(8,128)S(1)} %copy.27), channel_id=1, source_target_pairs={{0,1},{1,2},{2,3},{3,4},{4,5},{5,6},{6,7},{7,8},{8,9},{9,10},{10,1... | collective-permute-start | bytes 49160 | tf_op jit(solution)/shard_map/ppermute | solution.py:22
  61.6 8.3 %collective-permute-start.9 = (f32[32,128,1]{1,0,2:T(8,128)S(1)}, f32[32,128,1]{1,0,2:T(8,128)S(1)}, u32[]{:S(2)}, u32[]{:S(2)}) collective-permute-start(f32[32,128,1]{1,0,2:T(8,128)S(1)} %copy.28), channel_id=1, source_target_pairs={{1,0},{2,1},{3,2},{4,3},{5,4},{6,5},{7,6},{8,7},{9,8},{10,9},{11,1... | collective-permute-start | bytes 49160 | tf_op jit(solution)/shard_map/ppermute | solution.py:24
  72.8 11.1 %copy-start.31 = (f32[32,128,1]{2,0,1:T(8,128)S(1)}, f32[32,128,1]{2,0,1:T(8,128)}, u32[]{:S(2)}) copy-start(f32[32,128,1]{2,0,1:T(8,128)} %copy.30) | copy-start | bytes 49156
  73.8 6.3 %collective-permute-start.10 = (f32[32,1,130]{2,0,1:T(8,128)S(1)}, f32[32,1,130]{2,0,1:T(8,128)S(1)}, u32[]{:S(2)}, u32[]{:S(2)}) collective-permute-start(f32[32,1,130]{2,0,1:T(8,128)S(1)} %get-tuple-element.18), channel_id=1, source_target_pairs={{0,16},{16,32},{32,48},{48,64},{64,80},{80,96},{96,112},{1,17},{17... | collective-permute-start | bytes 49928 | tf_op jit(solution)/shard_map/ppermute | solution.py:22
  75.9 8.0 %collective-permute-start.11 = (f32[32,1,130]{2,0,1:T(8,128)S(1)}, f32[32,1,130]{2,0,1:T(8,128)S(1)}, u32[]{:S(2)}, u32[]{:S(2)}) collective-permute-start(f32[32,1,130]{2,0,1:T(8,128)S(1)} %get-tuple-element.19), channel_id=1, source_target_pairs={{16,0},{32,16},{48,32},{64,48},{80,64},{96,80},{112,96},{17,1},{33... | collective-permute-start | bytes 49928 | tf_op jit(solution)/shard_map/ppermute | solution.py:24
  96.0 10.3 %collective-permute-start.12 = (f32[32,128,1]{1,0,2:T(8,128)S(1)}, f32[32,128,1]{1,0,2:T(8,128)S(1)}, u32[]{:S(2)}, u32[]{:S(2)}) collective-permute-start(f32[32,128,1]{1,0,2:T(8,128)S(1)} %copy.32), channel_id=1, source_target_pairs={{0,1},{1,2},{2,3},{3,4},{4,5},{5,6},{6,7},{7,8},{8,9},{9,10},{10,1... | collective-permute-start | bytes 49160 | tf_op jit(solution)/shard_map/ppermute | solution.py:22
  98.7 10.5 %collective-permute-start.13 = (f32[32,128,1]{1,0,2:T(8,128)S(1)}, f32[32,128,1]{1,0,2:T(8,128)S(1)}, u32[]{:S(2)}, u32[]{:S(2)}) collective-permute-start(f32[32,128,1]{1,0,2:T(8,128)S(1)} %copy.33), channel_id=1, source_target_pairs={{1,0},{2,1},{3,2},{4,3},{5,4},{6,5},{7,6},{8,7},{9,8},{10,9},{11,1... | collective-permute-start | bytes 49160 | tf_op jit(solution)/shard_map/ppermute | solution.py:24
  113.0 8.2 %collective-permute-start.14 = (f32[32,1,130]{2,0,1:T(8,128)S(1)}, f32[32,1,130]{2,0,1:T(8,128)S(1)}, u32[]{:S(2)}, u32[]{:S(2)}) collective-permute-start(f32[32,1,130]{2,0,1:T(8,128)S(1)} %get-tuple-element.16), channel_id=1, source_target_pairs={{0,16},{16,32},{32,48},{48,64},{64,80},{80,96},{96,112},{1,17},{17... | collective-permute-start | bytes 49928 | tf_op jit(solution)/shard_map/ppermute | solution.py:22
  115.0 8.2 %collective-permute-start.15 = (f32[32,1,130]{2,0,1:T(8,128)S(1)}, f32[32,1,130]{2,0,1:T(8,128)S(1)}, u32[]{:S(2)}, u32[]{:S(2)}) collective-permute-start(f32[32,1,130]{2,0,1:T(8,128)S(1)} %get-tuple-element.17), channel_id=1, source_target_pairs={{16,0},{32,16},{48,32},{64,48},{80,64},{96,80},{112,96},{17,1},{33... | collective-permute-start | bytes 49928 | tf_op jit(solution)/shard_map/ppermute | solution.py:24
  144.3 9.9 %collective-permute-start.16 = (f32[32,128,1]{1,0,2:T(8,128)S(1)}, f32[32,128,1]{1,0,2:T(8,128)S(1)}, u32[]{:S(2)}, u32[]{:S(2)}) collective-permute-start(f32[32,128,1]{1,0,2:T(8,128)S(1)} %copy.37), channel_id=1, source_target_pairs={{0,1},{1,2},{2,3},{3,4},{4,5},{5,6},{6,7},{7,8},{8,9},{9,10},{10,1... | collective-permute-start | bytes 49160 | tf_op jit(solution)/shard_map/ppermute | solution.py:22
  147.0 10.1 %collective-permute-start.17 = (f32[32,128,1]{1,0,2:T(8,128)S(1)}, f32[32,128,1]{1,0,2:T(8,128)S(1)}, u32[]{:S(2)}, u32[]{:S(2)}) collective-permute-start(f32[32,128,1]{1,0,2:T(8,128)S(1)} %copy.38), channel_id=1, source_target_pairs={{1,0},{2,1},{3,2},{4,3},{5,4},{6,5},{7,6},{8,7},{9,8},{10,9},{11,1... | collective-permute-start | bytes 49160 | tf_op jit(solution)/shard_map/ppermute | solution.py:24
  161.0 8.4 %collective-permute-start.18 = (f32[32,1,130]{2,0,1:T(8,128)S(1)}, f32[32,1,130]{2,0,1:T(8,128)S(1)}, u32[]{:S(2)}, u32[]{:S(2)}) collective-permute-start(f32[32,1,130]{2,0,1:T(8,128)S(1)} %get-tuple-element.14), channel_id=1, source_target_pairs={{0,16},{16,32},{32,48},{48,64},{64,80},{80,96},{96,112},{1,17},{17... | collective-permute-start | bytes 49928 | tf_op jit(solution)/shard_map/ppermute | solution.py:22
  163.1 8.2 %collective-permute-start.19 = (f32[32,1,130]{2,0,1:T(8,128)S(1)}, f32[32,1,130]{2,0,1:T(8,128)S(1)}, u32[]{:S(2)}, u32[]{:S(2)}) collective-permute-start(f32[32,1,130]{2,0,1:T(8,128)S(1)} %get-tuple-element.15), channel_id=1, source_target_pairs={{16,0},{32,16},{48,32},{64,48},{80,64},{96,80},{112,96},{17,1},{33... | collective-permute-start | bytes 49928 | tf_op jit(solution)/shard_map/ppermute | solution.py:24
  196.9 8.1 %collective-permute-start.20 = (f32[32,128,1]{1,0,2:T(8,128)S(1)}, f32[32,128,1]{1,0,2:T(8,128)S(1)}, u32[]{:S(2)}, u32[]{:S(2)}) collective-permute-start(f32[32,128,1]{1,0,2:T(8,128)S(1)} %copy.47), channel_id=1, source_target_pairs={{0,1},{1,2},{2,3},{3,4},{4,5},{5,6},{6,7},{7,8},{8,9},{9,10},{10,1... | collective-permute-start | bytes 49160 | tf_op jit(solution)/shard_map/ppermute | solution.py:22
  199.7 8.3 %collective-permute-start.21 = (f32[32,128,1]{1,0,2:T(8,128)S(1)}, f32[32,128,1]{1,0,2:T(8,128)S(1)}, u32[]{:S(2)}, u32[]{:S(2)}) collective-permute-start(f32[32,128,1]{1,0,2:T(8,128)S(1)} %copy.48), channel_id=1, source_target_pairs={{1,0},{2,1},{3,2},{4,3},{5,4},{6,5},{7,6},{8,7},{9,8},{10,9},{11,1... | collective-permute-start | bytes 49160 | tf_op jit(solution)/shard_map/ppermute | solution.py:24
  210.9 11.6 %copy-start.8 = (f32[32,128,128]{2,0,1:T(8,128)S(1)}, f32[32,128,128]{2,0,1:T(8,128)}, u32[]{:S(2)}) copy-start(f32[32,128,128]{2,0,1:T(8,128)} %copy-done.7) | copy-start | bytes 6291460
  210.9 11.6 %copy-start.24 = (f32[32,128,1]{2,0,1:T(8,128)S(1)}, f32[32,128,1]{2,0,1:T(8,128)}, u32[]{:S(2)}) copy-start(f32[32,128,1]{2,0,1:T(8,128)} %copy.49) | copy-start | bytes 49156
  210.9 11.6 %copy-start.32 = (f32[32,128,1]{2,0,1:T(8,128)S(1)}, f32[32,128,1]{2,0,1:T(8,128)}, u32[]{:S(2)}) copy-start(f32[32,128,1]{2,0,1:T(8,128)} %copy.50) | copy-start | bytes 49156
  211.9 6.3 %collective-permute-start.22 = (f32[32,1,130]{2,0,1:T(8,128)S(1)}, f32[32,1,130]{2,0,1:T(8,128)S(1)}, u32[]{:S(2)}, u32[]{:S(2)}) collective-permute-start(f32[32,1,130]{2,0,1:T(8,128)S(1)} %get-tuple-element.12), channel_id=1, source_target_pairs={{0,16},{16,32},{32,48},{48,64},{64,80},{80,96},{96,112},{1,17},{17... | collective-permute-start | bytes 49928 | tf_op jit(solution)/shard_map/ppermute | solution.py:22
  214.5 7.9 %collective-permute-start.23 = (f32[32,1,130]{2,0,1:T(8,128)S(1)}, f32[32,1,130]{2,0,1:T(8,128)S(1)}, u32[]{:S(2)}, u32[]{:S(2)}) collective-permute-start(f32[32,1,130]{2,0,1:T(8,128)S(1)} %get-tuple-element.13), channel_id=1, source_target_pairs={{16,0},{32,16},{48,32},{64,48},{80,64},{96,80},{112,96},{17,1},{33... | collective-permute-start | bytes 49928 | tf_op jit(solution)/shard_map/ppermute | solution.py:24
  232.6 10.8 %collective-permute-start.24 = (f32[32,128,1]{1,0,2:T(8,128)S(1)}, f32[32,128,1]{1,0,2:T(8,128)S(1)}, u32[]{:S(2)}, u32[]{:S(2)}) collective-permute-start(f32[32,128,1]{1,0,2:T(8,128)S(1)} %copy.51), channel_id=1, source_target_pairs={{0,1},{1,2},{2,3},{3,4},{4,5},{5,6},{6,7},{7,8},{8,9},{9,10},{10,1... | collective-permute-start | bytes 49160 | tf_op jit(solution)/shard_map/ppermute | solution.py:22
  235.3 11.1 %collective-permute-start.25 = (f32[32,128,1]{1,0,2:T(8,128)S(1)}, f32[32,128,1]{1,0,2:T(8,128)S(1)}, u32[]{:S(2)}, u32[]{:S(2)}) collective-permute-start(f32[32,128,1]{1,0,2:T(8,128)S(1)} %copy.52), channel_id=1, source_target_pairs={{1,0},{2,1},{3,2},{4,3},{5,4},{6,5},{7,6},{8,7},{9,8},{10,9},{11,1... | collective-permute-start | bytes 49160 | tf_op jit(solution)/shard_map/ppermute | solution.py:24
  249.3 11.2 %copy-start.19 = (f32[32,128,1]{2,0,1:T(8,128)S(1)}, f32[32,128,1]{2,0,1:T(8,128)}, u32[]{:S(2)}) copy-start(f32[32,128,1]{2,0,1:T(8,128)} %copy.53) | copy-start | bytes 49156
  249.3 11.2 %copy-start.27 = (f32[32,128,1]{2,0,1:T(8,128)S(1)}, f32[32,128,1]{2,0,1:T(8,128)}, u32[]{:S(2)}) copy-start(f32[32,128,1]{2,0,1:T(8,128)} %copy.54) | copy-start | bytes 49156
  250.4 7.4 %collective-permute-start.26 = (f32[32,1,130]{2,0,1:T(8,128)S(1)}, f32[32,1,130]{2,0,1:T(8,128)S(1)}, u32[]{:S(2)}, u32[]{:S(2)}) collective-permute-start(f32[32,1,130]{2,0,1:T(8,128)S(1)} %get-tuple-element.10), channel_id=1, source_target_pairs={{0,16},{16,32},{32,48},{48,64},{64,80},{80,96},{96,112},{1,17},{17... | collective-permute-start | bytes 49928 | tf_op jit(solution)/shard_map/ppermute | solution.py:22
  252.5 7.9 %collective-permute-start.27 = (f32[32,1,130]{2,0,1:T(8,128)S(1)}, f32[32,1,130]{2,0,1:T(8,128)S(1)}, u32[]{:S(2)}, u32[]{:S(2)}) collective-permute-start(f32[32,1,130]{2,0,1:T(8,128)S(1)} %get-tuple-element.11), channel_id=1, source_target_pairs={{16,0},{32,16},{48,32},{64,48},{80,64},{96,80},{112,96},{17,1},{33... | collective-permute-start | bytes 49928 | tf_op jit(solution)/shard_map/ppermute | solution.py:24
  270.6 9.1 %collective-permute-start.28 = (f32[32,128,1]{1,0,2:T(8,128)S(1)}, f32[32,128,1]{1,0,2:T(8,128)S(1)}, u32[]{:S(2)}, u32[]{:S(2)}) collective-permute-start(f32[32,128,1]{1,0,2:T(8,128)S(1)} %copy.55), channel_id=1, source_target_pairs={{0,1},{1,2},{2,3},{3,4},{4,5},{5,6},{6,7},{7,8},{8,9},{9,10},{10,1... | collective-permute-start | bytes 49160 | tf_op jit(solution)/shard_map/ppermute | solution.py:22
  273.4 9.3 %collective-permute-start.29 = (f32[32,128,1]{1,0,2:T(8,128)S(1)}, f32[32,128,1]{1,0,2:T(8,128)S(1)}, u32[]{:S(2)}, u32[]{:S(2)}) collective-permute-start(f32[32,128,1]{1,0,2:T(8,128)S(1)} %copy.56), channel_id=1, source_target_pairs={{1,0},{2,1},{3,2},{4,3},{5,4},{6,5},{7,6},{8,7},{9,8},{10,9},{11,1... | collective-permute-start | bytes 49160 | tf_op jit(solution)/shard_map/ppermute | solution.py:24
  286.5 7.4 %collective-permute-start.30 = (f32[32,1,130]{2,0,1:T(8,128)S(1)}, f32[32,1,130]{2,0,1:T(8,128)S(1)}, u32[]{:S(2)}, u32[]{:S(2)}) collective-permute-start(f32[32,1,130]{2,0,1:T(8,128)S(1)} %get-tuple-element.8), channel_id=1, source_target_pairs={{0,16},{16,32},{32,48},{48,64},{64,80},{80,96},{96,112},{1,17},{17... | collective-permute-start | bytes 49928 | tf_op jit(solution)/shard_map/ppermute | solution.py:22
  288.7 7.9 %collective-permute-start.31 = (f32[32,1,130]{2,0,1:T(8,128)S(1)}, f32[32,1,130]{2,0,1:T(8,128)S(1)}, u32[]{:S(2)}, u32[]{:S(2)}) collective-permute-start(f32[32,1,130]{2,0,1:T(8,128)S(1)} %get-tuple-element.9), channel_id=1, source_target_pairs={{16,0},{32,16},{48,32},{64,48},{80,64},{96,80},{112,96},{17,1},{33... | collective-permute-start | bytes 49928 | tf_op jit(solution)/shard_map/ppermute | solution.py:24
  306.9 73.8 %collective-permute-start.32 = (f32[32,128,1]{1,0,2:T(8,128)S(1)}, f32[32,128,1]{1,0,2:T(8,128)}, u32[]{:S(2)}, u32[]{:S(2)}) collective-permute-start(f32[32,128,1]{1,0,2:T(8,128)S(1)} %copy.59), channel_id=1, source_target_pairs={{0,1},{1,2},{2,3},{3,4},{4,5},{5,6},{6,7},{7,8},{8,9},{9,10},{10,1... | collective-permute-start | bytes 49160 | tf_op jit(solution)/shard_map/ppermute | solution.py:22
  310.2 74.1 %collective-permute-start.33 = (f32[32,128,1]{1,0,2:T(8,128)}, f32[32,128,1]{1,0,2:T(8,128)}, u32[]{:S(2)}, u32[]{:S(2)}) collective-permute-start(f32[32,128,1]{1,0,2:T(8,128)} %copy.60), channel_id=1, source_target_pairs={{1,0},{2,1},{3,2},{4,3},{5,4},{6,5},{7,6},{8,7},{9,8},{10,9},{11,1... | collective-permute-start | bytes 49160 | tf_op jit(solution)/shard_map/ppermute | solution.py:24
  387.9 13.4 %copy-start.16 = (f32[32,128,128]{2,0,1:T(8,128)S(1)}, f32[32,128,128]{2,0,1:T(8,128)}, u32[]{:S(2)}) copy-start(f32[32,128,128]{2,0,1:T(8,128)} %copy-done.15) | copy-start | bytes 6291460
  387.9 13.4 %copy-start.18 = (f32[32,128,1]{2,0,1:T(8,128)S(1)}, f32[32,128,1]{2,0,1:T(8,128)}, u32[]{:S(2)}) copy-start(f32[32,128,1]{2,0,1:T(8,128)} %copy.61) | copy-start | bytes 49156
  387.9 13.4 %copy-start.26 = (f32[32,128,1]{2,0,1:T(8,128)S(1)}, f32[32,128,1]{2,0,1:T(8,128)}, u32[]{:S(2)}) copy-start(f32[32,128,1]{2,0,1:T(8,128)} %copy.62) | copy-start | bytes 49156
  388.9 7.3 %collective-permute-start.34 = (f32[32,1,130]{2,0,1:T(8,128)S(1)}, f32[32,1,130]{2,0,1:T(8,128)S(1)}, u32[]{:S(2)}, u32[]{:S(2)}) collective-permute-start(f32[32,1,130]{2,0,1:T(8,128)S(1)} %get-tuple-element.6), channel_id=1, source_target_pairs={{0,16},{16,32},{32,48},{48,64},{64,80},{80,96},{96,112},{1,17},{17... | collective-permute-start | bytes 49928 | tf_op jit(solution)/shard_map/ppermute | solution.py:22
  393.3 7.9 %collective-permute-start.35 = (f32[32,1,130]{2,0,1:T(8,128)S(1)}, f32[32,1,130]{2,0,1:T(8,128)S(1)}, u32[]{:S(2)}, u32[]{:S(2)}) collective-permute-start(f32[32,1,130]{2,0,1:T(8,128)S(1)} %get-tuple-element.7), channel_id=1, source_target_pairs={{16,0},{32,16},{48,32},{64,48},{80,64},{96,80},{112,96},{17,1},{33... | collective-permute-start | bytes 49928 | tf_op jit(solution)/shard_map/ppermute | solution.py:24
  (27 other events, 187.2 us)
where the time goes:
time: 416 us; the launch traced here: 408 us
  local copies, waits for them, and re-layouts  116 us (28%)
  starting transfers between devices  106 us (25%)
  other arithmetic  63.1 us (15%)
  blocking collectives  62.9 us (15%)
  matrix products  30.9 us (7%)
  waiting for transfers between devices  27.8 us (7%)
    ppermute x18, starting transfers between devices, padded_2(): lax.ppermute(head, axis, [((i + 1) % count, i) for i in range(ends)])  81.8 us
    psum x1, blocking collectives, local(): summed = lax.psum(weight_terms, ('lat', 'lon'))  62.9 us
    slice x17, local copies, waits for them, and re-layouts, padded_2(): lax.slice_in_dim(cells, cells.shape[dim] - width, cells.shape[dim], axis=...  44.4 us
    ppermute x18, waiting for transfers between devices, padded_2(): lax.ppermute(head, axis, [((i + 1) % count, i) for i in range(ends)])  27.7 us
    mul x9, other arithmetic, laplace(): return -scale_zero * neigh_sum(scale_one * padded, 1, 0)  24.9 us
    ppermute x18, starting transfers between devices, padded_2(): lax.ppermute(tail, axis, [(i, (i + 1) % count) for i in range(ends)])  24.2 us
    ppermute x8, local copies, waits for them, and re-layouts, padded_2(): lax.ppermute(tail, axis, [(i, (i + 1) % count) for i in range(ends)])  24 us
    ppermute x8, local copies, waits for them, and re-layouts, padded_2(): lax.ppermute(head, axis, [((i + 1) % count, i) for i in range(ends)])  23.6 us
  transfers between devices with their start and end apart: 36, of which 8 were waited for; matrix products, arithmetic and copies ran while one was open for 17% of the time, Pallas kernels for 0%

commit v1 on v0

v1 whole, which is shorter than its diff:
```python
import functools
import math

import jax
import jax.numpy as jnp
from jax import lax
from jax.experimental import pallas as pl
from jax.experimental.pallas import tpu as pltpu
from jax.sharding import PartitionSpec as P

K = 4
C = 32
B = 128
RG = 4
R = B // RG
H = 4
RE = R + 2 * H
CE = B + 16
CP = CE + 16
O = 16
F32 = jnp.float32
BF16 = jnp.bfloat16
NT = (((1,), (1,)), ((), ()))


def kernel(
    n_lat, n_lon,
    feat_hbm, cot_hbm, mask_hbm, w_hbm,
    out_hbm, wg_ref,
    feat_v, cot_v, mask_v, w_v, xf, cf, out_v,
    ya, yb, coef, scale, terms, gcat,
    mb, sm, vm, snat, wf, wb, eye, sel,
    pack, lrow, lcol, own, ar1, ar2,
    in_sem, out_sem, mask_send, mask_recv, halo_send, halo_recv,
    ar1_send, ar1_recv, ar2_send, ar2_recv,
):
    lat = lax.axis_index("lat")
    lon = lax.axis_index("lon")
    north, south = lax.rem(lat + n_lat - 1, n_lat), lax.rem(lat + 1, n_lat)
    west, east = lax.rem(lon + n_lon - 1, n_lon), lax.rem(lon + 1, n_lon)

    feat_in = pltpu.make_async_copy(feat_hbm, feat_v, in_sem.at[0])
    cot_in = pltpu.make_async_copy(cot_hbm, cot_v, in_sem.at[1])
    mask_in = pltpu.make_async_copy(mask_hbm, mask_v, in_sem.at[2])
    w_in = pltpu.make_async_copy(w_hbm, w_v, in_sem.at[3])
    mask_in.start()
    feat_in.start()
    w_in.start()
    cot_in.start()

    barrier = pltpu.get_barrier_semaphore()

    def greet(i, j):
        pl.semaphore_signal(
            barrier, inc=1, device_id=(i, j), device_id_type=pl.DeviceIdType.MESH
        )

    for i in (north, south):
        for j in (west, east):
            greet(i, j)

    def greet_lon(off, _):
        greet(lat, lax.rem(lon + off, n_lon))
        return 0

    def greet_lat(off, _):
        greet(lax.rem(lat + off, n_lat), lon)
        return 0

    lax.fori_loop(1, n_lon, greet_lon, 0)
    lax.fori_loop(1, n_lat, greet_lat, 0)

    row_i = lax.broadcasted_iota(jnp.int32, (B, B), 0)
    col_i = lax.broadcasted_iota(jnp.int32, (B, B), 1)
    eye[...] = (row_i == col_i).astype(F32).astype(BF16)
    sel_r = lax.broadcasted_iota(jnp.int32, (CE, 2 * B), 0)
    sel_c = lax.broadcasted_iota(jnp.int32, (CE, 2 * B), 1)
    inside = (sel_r >= 8) & (sel_r < 8 + B) & (sel_c == sel_r - 8)
    left = (sel_r < 8) & (sel_c == 2 * B - 8 + sel_r)
    right = (sel_r >= 8 + B) & (sel_c == sel_r - 8)
    sel[...] = (inside | left | right).astype(F32).astype(BF16)

    mask_in.wait()
    mb[1, 8 : 8 + B, :] = mask_v[...].astype(F32)
    pl.semaphore_wait(barrier, 4 + (n_lon - 1) + (n_lat - 1))

    def remote(src, dst, send, recv, i, j):
        return pltpu.make_async_remote_copy(
            src_ref=src, dst_ref=dst, send_sem=send, recv_sem=recv,
            device_id=(i, j), device_id_type=pl.DeviceIdType.MESH,
        )

    mid, top, bottom = pl.ds(8, B), pl.ds(8, 8), pl.ds(B, 8)
    above, below = pl.ds(0, 8), pl.ds(8 + B, 8)
    mask_plan = (
        (mid, 0, mid, lat, east),
        (mid, 2, mid, lat, west),
        (bottom, 1, above, south, lon),
        (top, 1, below, north, lon),
        (bottom, 0, above, south, east),
        (bottom, 2, above, south, west),
        (top, 0, below, north, east),
        (top, 2, below, north, west),
    )
    mask_copies = [
        remote(mb.at[1, src], mb.at[slot, dst], mask_send.at[n], mask_recv.at[n], i, j)
        for n, (src, slot, dst, i, j) in enumerate(mask_plan)
    ]
    for copy in mask_copies:
        copy.start()

    lane = lax.broadcasted_iota(jnp.int32, (B, B), 1)

    def halo_copies(phase, y):
        plan = (
            (pack.at[phase, 0], lrow.at[phase, 0, mid], south, lon),
            (pack.at[phase, 1], lrow.at[phase, 1, mid], north, lon),
            (pack.at[phase, 0, pl.ds(B - 8, 8)], lrow.at[phase, 0, above], south, east),
            (pack.at[phase, 0, pl.ds(0, 8)], lrow.at[phase, 0, below], south, west),
            (pack.at[phase, 1, pl.ds(B - 8, 8)], lrow.at[phase, 1, above], north, east),
            (pack.at[phase, 1, pl.ds(0, 8)], lrow.at[phase, 1, below], north, west),
            (y.at[pl.ds(H, R), pl.ds(O + B - 8, 8)], lcol.at[phase, 0], lat, east),
            (y.at[pl.ds(H, R), pl.ds(O, 8)], lcol.at[phase, 1], lat, west),
        )
        return [
            remote(src, dst, halo_send.at[phase, n], halo_recv.at[phase, n], i, j)
            for n, (src, dst, i, j) in enumerate(plan)
        ]

    def pack_rows(phase, y):
        last, first = None, None
        for i in range(H):
            a = pltpu.roll(y[H + R - H + i, O : O + B, :], (32 * i + 32) % 128, 1)
            b = pltpu.roll(y[H + i, O : O + B, :], (32 * i) % 128, 1)
            here = (lane >= 32 * i) & (lane < 32 * i + 32)
            last = a if last is None else jnp.where(here, a, last)
            first = b if first is None else jnp.where(here, b, first)
        pack[phase, 0] = last
        pack[phase, 1] = first

    feat_in.wait()

    def widen(src, dst):
        def body(c, _):
            dst[pl.ds(pl.multiple_of(c * B, B), B), :] = src[c].astype(F32)
            return 0

        lax.fori_loop(0, C, body, 0)

    def rows_of(flat, r):
        return jnp.concatenate(
            [flat[pl.ds(R * g + r, C, stride=B), :] for g in range(RG)], axis=0
        )

    widen(feat_v, xf)

    def turn(r):
        x = rows_of(xf, r).astype(BF16)
        yb[H + r, O : O + B, :] = lax.dot_general(
            eye[...], x, NT, preferred_element_type=F32
        )

    def turn_edge(i, _):
        turn(i + (R - 2 * H) * (i // H))
        return 0

    def turn_inner(i, _):
        turn(i)
        return 0

    lax.fori_loop(0, 2 * H, turn_edge, 0)
    first_halo = halo_copies(0, yb)
    pack_rows(0, yb)
    for copy in first_halo[:6]:
        copy.start()
    lax.fori_loop(H, R - H, turn_inner, 0)
    for copy in first_halo[6:]:
        copy.start()

    w_in.wait()
    block = (row_i // C) == (col_i // C)
    for k in range(K + 1):
        one = w_v[k].astype(F32)
        wide = jnp.concatenate([one] * RG, axis=1)
        full = jnp.where(block, jnp.concatenate([wide] * RG, axis=0), 0.0)
        wb[:, k * B : (k + 1) * B] = full.astype(BF16)
        wf[:, k * B : (k + 1) * B] = full.T.astype(BF16)

    for copy in mask_copies:
        copy.wait()
    north_ok = (lat > 0).astype(F32)
    south_ok = (lat < n_lat - 1).astype(F32)
    lane_e = lax.broadcasted_iota(jnp.int32, (CE, B), 1)
    row_e = lax.broadcasted_iota(jnp.int32, (CE, B), 0)
    ok = jnp.where(row_e < 8, north_ok, jnp.where(row_e >= 8 + B, south_ok, 1.0))
    sm[...] = jnp.zeros_like(sm)
    sm[0, 8 : 8 + CE, :] = mb[1] * ok
    sm[1, 8 : 8 + CE, :] = jnp.where(lane_e < 64, mb[2], mb[0]) * ok

    def ring(main, side, shift, edge):
        m, s = pltpu.roll(main, shift, 1), pltpu.roll(side, shift, 1)
        at = lane_e == edge
        return jnp.where(at, s, m), jnp.where(at, m, s)

    here = [sm[t, 8 : 8 + CE, :] for t in range(2)]
    up = [sm[t, 7 : 7 + CE, :] for t in range(2)]
    down = [sm[t, 9 : 9 + CE, :] for t in range(2)]
    from_left = ring(here[0] + down[0], here[1] + down[1], 1, 0)
    from_right = ring(here[0] + up[0], here[1] + up[1], B - 1, B - 1)
    for t in range(2):
        degree = from_left[t] + from_right[t] + up[t] + down[t]
        vm[:, t * B : (t + 1) * B] = here[t] * jnp.maximum(degree, 1.0)
        if t == 0:
            snat[...] = jnp.sqrt(jnp.maximum(degree, 1.0)[8 : 8 + B])

    def spread(r, _):
        rows = jnp.concatenate(
            [
                jnp.broadcast_to(vm[pl.ds(8 - H + R * g + r, 1), :], (C, 2 * B))
                for g in range(RG)
            ],
            axis=0,
        )
        v = lax.dot_general(sel[...], rows.astype(BF16), NT, preferred_element_type=F32)
        m = jnp.maximum(v, 1.0)
        rs = lax.rsqrt(m)
        coef[r] = jnp.where(v > 0.5, -2.0 * rs * rs, 0.0)
        scale[r] = m * rs
        return 0

    lax.fori_loop(0, RE, spread, 0)

    def assemble(phase, y, ok_north, ok_south):
        def sides(r, _):
            y[H + r, O - 8 : O, :] = lcol[phase, 0, r]
            y[H + r, O + B : O + B + 8, :] = lcol[phase, 1, r]
            return 0

        lax.fori_loop(0, R, sides, 0)
        for i in range(H):
            own_up = pltpu.roll(y[R + i, O - 8 : O + B + 8, :], 32, 1)
            far_up = pltpu.roll(lrow[phase, 0], (B - 32 * i) % B, 1) * ok_north
            y[i, O - 8 : O + B + 8, :] = jnp.where(lane_e < 32, far_up, own_up)
            own_down = pltpu.roll(y[H + i, O - 8 : O + B + 8, :], B - 32, 1)
            far_down = pltpu.roll(lrow[phase, 1], (96 - 32 * i) % B, 1) * ok_south
            y[H + R + i, O - 8 : O + B + 8, :] = jnp.where(
                lane_e >= 96, far_down, own_down
            )

    def keep(k, r, value):
        terms[pl.ds(pl.multiple_of(r * B, B), B), k * B : (k + 1) * B] = value.astype(BF16)

    def step(src, dst, k, scaled):
        reach = K - k
        first, count = (O - 8, CE) if reach else (O, B)
        skip = O - first

        def sums(r):
            mid_ = src[r, first : first + count, :]
            low = src[r, first - 1 : first - 1 + count, :]
            high = src[r, first + 1 : first + 1 + count, :]
            return mid_ + high, low + high, mid_ + low

        def advance(r, carried):
            e0, e1, f1 = carried
            e2, f2, h2 = sums(r + 1)
            a = coef[r, first - O + 8 : first - O + 8 + count, :]
            total = a * (e0 + f1 + h2)
            if k == 1:
                value = 0.5 * total
            else:
                value = total - dst[r, first : first + count, :]
            dst[r, first : first + count, :] = value
            return (e1, e2, f2), value

        def outer(r, carried):
            return advance(r, carried)[0]

        def inner(r, carried):
            carried, value = advance(r, carried)
            value = value[skip : skip + B]
            if scaled:
                value = value * scale[r, 8 : 8 + B, :]
            keep(k, r - H, value)
            return carried

        low = H - reach
        e0 = sums(low - 1)[0]
        e1, f1, _ = sums(low)
        carried = (e0, e1, f1)
        if reach:
            carried = lax.fori_loop(low, H, outer, carried)
        carried = lax.fori_loop(H, H + R, inner, carried)
        if reach:
            lax.fori_loop(H + R, H + R + reach, outer, carried)

    for copy in first_halo:
        copy.wait()
    assemble(0, yb, 1.0, 1.0)

    def start_row(r, _):
        x = yb[r, O - 8 : O + B + 8, :]
        ya[r, O - 8 : O + B + 8, :] = (-0.5 * coef[r] * scale[r]) * x
        return 0

    lax.fori_loop(0, RE, start_row, 0)

    def keep_first(r, _):
        keep(0, r, ya[H + r, O : O + B, :] * scale[H + r, 8 : 8 + B, :])
        return 0

    lax.fori_loop(0, R, keep_first, 0)
    step(ya, yb, 1, True)
    step(yb, ya, 2, True)
    step(ya, yb, 3, True)
    step(yb, ya, 4, True)

    cot_in.wait()
    widen(cot_v, cf)

    def mix(r):
        t = terms[pl.ds(pl.multiple_of(r * B, B), B), :]
        mixed = lax.dot_general(wf[...], t, NT, preferred_element_type=F32)
        act = jnp.tanh(mixed)
        grad = (rows_of(cf, r) * (1.0 - act * act)).astype(BF16)
        gcat[:, pl.ds(pl.multiple_of(r * B, B), B)] = grad
        turned = lax.dot_general(eye[...], grad, NT, preferred_element_type=F32)
        w = -0.5 * coef[H + r, 8 : 8 + B, :] * scale[H + r, 8 : 8 + B, :]
        ya[H + r, O : O + B, :] = w * turned

    def mix_edge(i, _):
        mix(i + (R - 2 * H) * (i // H))
        return 0

    def mix_inner(i, _):
        mix(i)
        return 0

    lax.fori_loop(0, 2 * H, mix_edge, 0)
    second_halo = halo_copies(1, ya)
    pack_rows(1, ya)
    for copy in second_halo[:6]:
        copy.start()
    lax.fori_loop(H, R - H, mix_inner, 0)
    for copy in second_halo[6:]:
        copy.start()

    chunk = 8 * B
    acc = None
    for n in range(R * B // chunk):
        part = jnp.dot(
            gcat[:, n * chunk : (n + 1) * chunk],
            terms[n * chunk : (n + 1) * chunk, :],
            preferred_element_type=F32,
        )
        acc = part if acc is None else acc + part
    lane_c = lax.broadcasted_iota(jnp.int32, (C, B), 1) // C
    folded = []
    for k in range(K + 1):
        tot = None
        for g in range(RG):
            piece = acc[g * C : (g + 1) * C, k * B : (k + 1) * B]
            tot = piece if tot is None else jnp.where(lane_c == g, piece, tot)
        tot = tot + pltpu.roll(tot, 64, 1)
        tot = tot + pltpu.roll(tot, 32, 1)
        folded.append(tot)
    head = folded[0]
    for k in range(1, K):
        head = jnp.where(lane_c == k, folded[k], head)
    tail = folded[K][0:8]
    for g in range(1, RG):
        tail = jnp.where(lane_c[0:8] == g, folded[K][8 * g : 8 * g + 8], tail)
    grid_cells = n_lat * n_lon * B * B
    own[0, 0:C, :] = head * (1.0 / math.sqrt(grid_cells))
    own[0, C : C + 8, :] = tail * (1.0 / math.sqrt(grid_cells))

    def lon_copy(off):
        return remote(
            own.at[0], ar1.at[lon], ar1_send.at[off], ar1_recv.at[lon],
            lat, lax.rem(lon + off, n_lon),
        )

    def lon_wait(off):
        q = lax.rem(lon + n_lon - off, n_lon)
        return remote(own.at[0], ar1.at[q], ar1_send.at[off], ar1_recv.at[q], lat, q)

    def lat_copy(off):
        return remote(
            own.at[1], ar2.at[lat], ar2_send.at[off], ar2_recv.at[lat],
            lax.rem(lat + off, n_lat), lon,
        )

    def lat_wait(off):
        q = lax.rem(lat + n_lat - off, n_lat)
        return remote(own.at[1], ar2.at[q], ar2_send.at[off], ar2_recv.at[q], q, lon)

    def run(count, act):
        def body(off, _):
            act(off)
            return 0

        lax.fori_loop(1, count, body, 0)

    run(n_lon, lambda off: lon_copy(off).start())
    ar1[lon] = own[0]

    for copy in second_halo:
        copy.wait()
    assemble(1, ya, north_ok, south_ok)

    def keep_grad(r, _):
        keep(0, r, ya[H + r, O : O + B, :])
        return 0

    lax.fori_loop(0, R, keep_grad, 0)
    step(ya, yb, 1, False)
    step(yb, ya, 2, False)

    run(n_lon, lambda off: lon_wait(off).wait())
    total = ar1[0]
    for q in range(1, n_lon):
        total = total + ar1[q]
    own[1] = total
    run(n_lat, lambda off: lat_copy(off).start())
    ar2[lat] = total

    step(ya, yb, 3, False)
    step(yb, ya, 4, False)

    def finish(r, _):
        t = terms[pl.ds(pl.multiple_of(r * B, B), B), :]
        res = lax.dot_general(wb[...], t, NT, preferred_element_type=F32)
        for g in range(RG):
            s = jnp.broadcast_to(snat[pl.ds(R * g + r, 1), :], (C, B))
            xf[pl.ds(R * g + r, C, stride=B), :] = res[g * C : (g + 1) * C] * s
        return 0

    lax.fori_loop(0, R, finish, 0)

    def narrow(c, _):
        out_v[c] = xf[pl.ds(pl.multiple_of(c * B, B), B), :].astype(BF16)
        return 0

    lax.fori_loop(0, C, narrow, 0)
    out_copy = pltpu.make_async_copy(out_v, out_hbm, out_sem)
    out_copy.start()

    run(n_lat, lambda off: lat_wait(off).wait())
    total = ar2[0]
    for q in range(1, n_lat):
        total = total + ar2[q]
    flat = total[0:C].T
    for k in range(K):
        wg_ref[k] = flat[k * C : (k + 1) * C, :]
    last = total[C : C + 8]
    last = jnp.concatenate(
        [last if g == 0 else pltpu.roll(last, B - C * g, 1) for g in range(RG)], axis=0
    )
    wg_ref[K] = last.T[0:C, :]
    out_copy.wait()


def solution(mesh):
    n_lat, n_lon = mesh.shape["lat"], mesh.shape["lon"]
    hbm = pl.BlockSpec(memory_space=pl.ANY)
    sem = pltpu.SemaphoreType.DMA

    def local(features, cotangent, sea_mask, weights):
        return pl.pallas_call(
            functools.partial(kernel, n_lat, n_lon),
            out_shape=(
                jax.ShapeDtypeStruct((C, B, B), BF16),
                jax.ShapeDtypeStruct((K + 1, C, C), F32),
            ),
            in_specs=[hbm] * 4,
            out_specs=(hbm, pl.BlockSpec(memory_space=pltpu.VMEM)),
            scratch_shapes=[
                pltpu.VMEM((C, B, B), BF16),
                pltpu.VMEM((C, B, B), BF16),
                pltpu.VMEM((B, B), jnp.int32),
                pltpu.VMEM((K + 1, C, C), BF16),
                pltpu.VMEM((C * B, B), F32),
                pltpu.VMEM((C * B, B), F32),
                pltpu.VMEM((C, B, B), BF16),
                pltpu.VMEM((RE, CP, B), F32),
                pltpu.VMEM((RE, CP, B), F32),
                pltpu.VMEM((RE, CE, B), F32),
                pltpu.VMEM((RE, CE, B), F32),
                pltpu.VMEM((R * B, (K + 1) * B), BF16),
                pltpu.VMEM((B, R * B), BF16),
                pltpu.VMEM((3, CE, B), F32),
                pltpu.VMEM((2, CP, B), F32),
                pltpu.VMEM((CE, 2 * B), F32),
                pltpu.VMEM((B, B), F32),
                pltpu.VMEM((B, (K + 1) * B), BF16),
                pltpu.VMEM((B, (K + 1) * B), BF16),
                pltpu.VMEM((B, B), BF16),
                pltpu.VMEM((CE, 2 * B), BF16),
                pltpu.VMEM((2, 2, B, B), F32),
                pltpu.VMEM((2, 2, CE, B), F32),
                pltpu.VMEM((2, 2, R, 8, B), F32),
                pltpu.VMEM((2, C + 8, B), F32),
                pltpu.VMEM((n_lon, C + 8, B), F32),
                pltpu.VMEM((n_lat, C + 8, B), F32),
                sem((4,)), sem(()), sem((8,)), sem((8,)), sem((2, 8)), sem((2, 8)),
                sem((n_lon,)), sem((n_lon,)), sem((n_lat,)), sem((n_lat,)),
            ],
            compiler_params=pltpu.CompilerParams(
                collective_id=0, has_side_effects=True, vmem_limit_bytes=56 << 20
            ),
        )(features, cotangent, sea_mask, weights)

    placed = (P(None, "lat", "lon"), P(None, "lat", "lon"), P("lat", "lon"), P())
    return jax.shard_map(
        local, mesh=mesh, in_specs=placed, out_specs=(P(None, "lat", "lon"), P()), check_vma=False
    )
```

time: 416 us -> 68.1 us (0.16)
  the two profiles are of different devices: /device:TPU:96 before, /device:TPU:1 now
where the time goes in v1:
time: 68.1 us; the launch traced here: 67.9 us
  Pallas kernels  64.2 us (94%)
  local copies, waits for them, and re-layouts  2.98 us (4%)
    pallas_call x1, Pallas kernels, local(): pl.pallas_call(functools.partial(kernel, n_lat, n_lon), out_shape=(jax.Sh...  64.2 us
    unnamed x4, local copies, waits for them, and re-layouts  2.98 us

profile of v1, /device:TPU:1, one launch (start us, length us, event | category | flops | bytes accessed | tf_op | source)
XLA Modules:
  0.0 67.9 jit_solution(17793391082463338566)
XLA Ops:
  0.6 64.2 %shard_map.59 = (bf16[32,128,128]{2,1,0:T(8,128)(2,1)}, f32[5,32,32]{2,1,0:T(8,128)}) custom-call(bf16[32,128,128]{2,1,0:T(8,128)(2,1)} %feat_hbm.1, bf16[32,128,128]{2,1,0:T(8,128)(2,1)} %cot_hbm.1, s32[128,128]{1,0:T(8,128)} %mask_hbm.1, bf16[5,32,32]{2,1,0:T(8,128)(2,1)} %w_hbm.1), custom_call_target="tpu_custom_call" | custom-call | tf_op jit(solution)/shard_map/pallas_call | solution.py:469
  64.9 0.0 copy-start
  64.9 2.3 %copy.8 = bf16[32,128,128]{2,1,0:T(8,128)(2,1)} copy(bf16[32,128,128]{2,1,0:T(8,128)(2,1)} %get-tuple-element.4) | data formatting | bytes 2097152
  67.2 0.0 copy-done
  67.2 0.6 copy.9
Async XLA Ops:
  64.9 2.4 %copy-start = (f32[5,32,32]{2,1,0:T(8,128)S(1)}, f32[5,32,32]{2,1,0:T(8,128)}, u32[]{:S(2)}) copy-start(f32[5,32,32]{2,1,0:T(8,128)} %get-tuple-element.5) | copy-start | bytes 61444

commit v2 on v1

--- a/solution.py
+++ b/solution.py
@@ -29,7 +29,7 @@
     out_hbm, wg_ref,
     feat_v, cot_v, mask_v, w_v, xf, cf, out_v,
     ya, yb, coef, scale, terms, gcat,
-    mb, sm, vm, snat, wf, wb, eye, sel,
+    mb, sm, vm, snat, wf, wb, sel,
     pack, lrow, lcol, own, ar1, ar2,
     in_sem, out_sem, mask_send, mask_recv, halo_send, halo_recv,
     ar1_send, ar1_recv, ar2_send, ar2_recv,
@@ -72,7 +72,6 @@
 
     row_i = lax.broadcasted_iota(jnp.int32, (B, B), 0)
     col_i = lax.broadcasted_iota(jnp.int32, (B, B), 1)
-    eye[...] = (row_i == col_i).astype(F32).astype(BF16)
     sel_r = lax.broadcasted_iota(jnp.int32, (CE, 2 * B), 0)
     sel_c = lax.broadcasted_iota(jnp.int32, (CE, 2 * B), 1)
     inside = (sel_r >= 8) & (sel_r < 8 + B) & (sel_c == sel_r - 8)
@@ -145,7 +144,7 @@
             dst[pl.ds(pl.multiple_of(c * B, B), B), :] = src[c].astype(F32)
             return 0
 
-        lax.fori_loop(0, C, body, 0)
+        lax.fori_loop(0, C, body, 0, unroll=4)
 
     def rows_of(flat, r):
         return jnp.concatenate(
@@ -155,10 +154,7 @@
     widen(feat_v, xf)
 
     def turn(r):
-        x = rows_of(xf, r).astype(BF16)
-        yb[H + r, O : O + B, :] = lax.dot_general(
-            eye[...], x, NT, preferred_element_type=F32
-        )
+        yb[H + r, O : O + B, :] = rows_of(xf, r).T
 
     def turn_edge(i, _):
         turn(i + (R - 2 * H) * (i // H))
@@ -168,12 +164,12 @@
         turn(i)
         return 0
 
-    lax.fori_loop(0, 2 * H, turn_edge, 0)
+    lax.fori_loop(0, 2 * H, turn_edge, 0, unroll=8)
     first_halo = halo_copies(0, yb)
     pack_rows(0, yb)
     for copy in first_halo[:6]:
         copy.start()
-    lax.fori_loop(H, R - H, turn_inner, 0)
+    lax.fori_loop(H, R - H, turn_inner, 0, unroll=8)
     for copy in first_halo[6:]:
         copy.start()
 
@@ -213,10 +209,11 @@
         if t == 0:
             snat[...] = jnp.sqrt(jnp.maximum(degree, 1.0)[8 : 8 + B])
 
-    def spread(r, _):
+    def spread(p, _):
         rows = jnp.concatenate(
             [
-                jnp.broadcast_to(vm[pl.ds(8 - H + R * g + r, 1), :], (C, 2 * B))
+                jnp.broadcast_to(vm[pl.ds(8 - H + R * g + 2 * p + j, 1), :], (C, 2 * B))
+                for j in range(2)
                 for g in range(RG)
             ],
             axis=0,
@@ -224,11 +221,13 @@
         v = lax.dot_general(sel[...], rows.astype(BF16), NT, preferred_element_type=F32)
         m = jnp.maximum(v, 1.0)
         rs = lax.rsqrt(m)
-        coef[r] = jnp.where(v > 0.5, -2.0 * rs * rs, 0.0)
-        scale[r] = m * rs
-        return 0
-
-    lax.fori_loop(0, RE, spread, 0)
+        a, s = jnp.where(v > 0.5, -2.0 * rs * rs, 0.0), m * rs
+        for j in range(2):
+            coef[2 * p + j] = a[:, j * B : (j + 1) * B]
+            scale[2 * p + j] = s[:, j * B : (j + 1) * B]
+        return 0
+
+    lax.fori_loop(0, RE // 2, spread, 0, unroll=4)
 
     def assemble(phase, y, ok_north, ok_south):
         def sides(r, _):
@@ -236,7 +235,7 @@
             y[H + r, O + B : O + B + 8, :] = lcol[phase, 1, r]
             return 0
 
-        lax.fori_loop(0, R, sides, 0)
+        lax.fori_loop(0, R, sides, 0, unroll=4)
         for i in range(H):
             own_up = pltpu.roll(y[R + i, O - 8 : O + B + 8, :], 32, 1)
             far_up = pltpu.roll(lrow[phase, 0], (B - 32 * i) % B, 1) * ok_north
@@ -253,24 +252,30 @@
     def step(src, dst, k, scaled):
         reach = K - k
         first, count = (O - 8, CE) if reach else (O, B)
-        skip = O - first
+        size = 48 if reach else 64
+        for at in range(0, count, size):
+            step_block(src, dst, k, scaled, first + at, size)
+
+    def step_block(src, dst, k, scaled, first, size):
+        reach = K - k
+        lo, hi = max(first, O), min(first + size, O + B)
 
         def sums(r):
-            mid_ = src[r, first : first + count, :]
-            low = src[r, first - 1 : first - 1 + count, :]
-            high = src[r, first + 1 : first + 1 + count, :]
+            mid_ = src[r, first : first + size, :]
+            low = src[r, first - 1 : first - 1 + size, :]
+            high = src[r, first + 1 : first + 1 + size, :]
             return mid_ + high, low + high, mid_ + low
 
         def advance(r, carried):
             e0, e1, f1 = carried
             e2, f2, h2 = sums(r + 1)
-            a = coef[r, first - O + 8 : first - O + 8 + count, :]
+            a = coef[r, first - O + 8 : first - O + 8 + size, :]
             total = a * (e0 + f1 + h2)
             if k == 1:
                 value = 0.5 * total
             else:
-                value = total - dst[r, first : first + count, :]
-            dst[r, first : first + count, :] = value
+                value = total - dst[r, first : first + size, :]
+            dst[r, first : first + size, :] = value
             return (e1, e2, f2), value
 
         def outer(r, carried):
@@ -278,10 +283,11 @@
 
         def inner(r, carried):
             carried, value = advance(r, carried)
-            value = value[skip : skip + B]
+            value = value[lo - first : hi - first]
             if scaled:
-                value = value * scale[r, 8 : 8 + B, :]
-            keep(k, r - H, value)
+                value = value * scale[r, lo - O + 8 : hi - O + 8, :]
+            at = pl.multiple_of((r - H) * B + lo - O, 8)
+            terms[pl.ds(at, hi - lo), k * B : (k + 1) * B] = value.astype(BF16)
             return carried
 
         low = H - reach
@@ -289,10 +295,10 @@
         e1, f1, _ = sums(low)
         carried = (e0, e1, f1)
         if reach:
-            carried = lax.fori_loop(low, H, outer, carried)
-        carried = lax.fori_loop(H, H + R, inner, carried)
+            carried = lax.fori_loop(low, H, outer, carried, unroll=reach)
+        carried = lax.fori_loop(H, H + R, inner, carried, unroll=8)
         if reach:
-            lax.fori_loop(H + R, H + R + reach, outer, carried)
+            lax.fori_loop(H + R, H + R + reach, outer, carried, unroll=reach)
 
     for copy in first_halo:
         copy.wait()
@@ -303,13 +309,13 @@
         ya[r, O - 8 : O + B + 8, :] = (-0.5 * coef[r] * scale[r]) * x
         return 0
 
-    lax.fori_loop(0, RE, start_row, 0)
+    lax.fori_loop(0, RE, start_row, 0, unroll=4)
 
     def keep_first(r, _):
         keep(0, r, ya[H + r, O : O + B, :] * scale[H + r, 8 : 8 + B, :])
         return 0
 
-    lax.fori_loop(0, R, keep_first, 0)
+    lax.fori_loop(0, R, keep_first, 0, unroll=4)
     step(ya, yb, 1, True)
     step(yb, ya, 2, True)
     step(ya, yb, 3, True)
@@ -318,30 +324,42 @@
     cot_in.wait()
     widen(cot_v, cf)
 
-    def mix(r):
-        t = terms[pl.ds(pl.multiple_of(r * B, B), B), :]
-        mixed = lax.dot_general(wf[...], t, NT, preferred_element_type=F32)
+    def mix(p):
+        at = pl.ds(pl.multiple_of(2 * p * B, 2 * B), 2 * B)
+        mixed = lax.dot_general(wf[...], terms[at, :], NT, preferred_element_type=F32)
         act = jnp.tanh(mixed)
-        grad = (rows_of(cf, r) * (1.0 - act * act)).astype(BF16)
-        gcat[:, pl.ds(pl.multiple_of(r * B, B), B)] = grad
-        turned = lax.dot_general(eye[...], grad, NT, preferred_element_type=F32)
+        cot = jnp.concatenate([rows_of(cf, 2 * p), rows_of(cf, 2 * p + 1)], axis=1)
+        gcat[:, at] = (cot * (1.0 - act * act)).astype(BF16)
+
+    def turn_grad(r):
+        grad = gcat[:, pl.ds(pl.multiple_of(r * B, B), B)].astype(F32)
         w = -0.5 * coef[H + r, 8 : 8 + B, :] * scale[H + r, 8 : 8 + B, :]
-        ya[H + r, O : O + B, :] = w * turned
+        ya[H + r, O : O + B, :] = w * grad.T
 
     def mix_edge(i, _):
-        mix(i + (R - 2 * H) * (i // H))
+        mix(i + (R // 2 - H) * (i // (H // 2)))
         return 0
 
     def mix_inner(i, _):
         mix(i)
         return 0
 
-    lax.fori_loop(0, 2 * H, mix_edge, 0)
+    def grad_edge(i, _):
+        turn_grad(i + (R - 2 * H) * (i // H))
+        return 0
+
+    def grad_inner(i, _):
+        turn_grad(i)
+        return 0
+
+    lax.fori_loop(0, H, mix_edge, 0, unroll=H)
+    lax.fori_loop(0, 2 * H, grad_edge, 0, unroll=8)
     second_halo = halo_copies(1, ya)
     pack_rows(1, ya)
     for copy in second_halo[:6]:
         copy.start()
-    lax.fori_loop(H, R - H, mix_inner, 0)
+    lax.fori_loop(H // 2, R // 2 - H // 2, mix_inner, 0, unroll=4)
+    lax.fori_loop(H, R - H, grad_inner, 0, unroll=8)
     for copy in second_halo[6:]:
         copy.start()
 
@@ -412,7 +430,7 @@
         keep(0, r, ya[H + r, O : O + B, :])
         return 0
 
-    lax.fori_loop(0, R, keep_grad, 0)
+    lax.fori_loop(0, R, keep_grad, 0, unroll=4)
     step(ya, yb, 1, False)
     step(yb, ya, 2, False)
 
@@ -427,21 +445,24 @@
     step(ya, yb, 3, False)
     step(yb, ya, 4, False)
 
-    def finish(r, _):
-        t = terms[pl.ds(pl.multiple_of(r * B, B), B), :]
+    def finish(p, _):
+        t = terms[pl.ds(pl.multiple_of(2 * p * B, 2 * B), 2 * B), :]
         res = lax.dot_general(wb[...], t, NT, preferred_element_type=F32)
-        for g in range(RG):
-            s = jnp.broadcast_to(snat[pl.ds(R * g + r, 1), :], (C, B))
-            xf[pl.ds(R * g + r, C, stride=B), :] = res[g * C : (g + 1) * C] * s
-        return 0
-
-    lax.fori_loop(0, R, finish, 0)
+        for j in range(2):
+            for g in range(RG):
+                row = R * g + 2 * p + j
+                s = jnp.broadcast_to(snat[pl.ds(row, 1), :], (C, B))
+                part = res[g * C : (g + 1) * C, j * B : (j + 1) * B]
+                xf[pl.ds(row, C, stride=B), :] = part * s
+        return 0
+
+    lax.fori_loop(0, R // 2, finish, 0, unroll=4)
 
     def narrow(c, _):
         out_v[c] = xf[pl.ds(pl.multiple_of(c * B, B), B), :].astype(BF16)
         return 0
 
-    lax.fori_loop(0, C, narrow, 0)
+    lax.fori_loop(0, C, narrow, 0, unroll=4)
     out_copy = pltpu.make_async_copy(out_v, out_hbm, out_sem)
     out_copy.start()
 
@@ -494,7 +515,6 @@
                 pltpu.VMEM((B, B), F32),
                 pltpu.VMEM((B, (K + 1) * B), BF16),
                 pltpu.VMEM((B, (K + 1) * B), BF16),
-                pltpu.VMEM((B, B), BF16),
                 pltpu.VMEM((CE, 2 * B), BF16),
                 pltpu.VMEM((2, 2, B, B), F32),
                 pltpu.VMEM((2, 2, CE, B), F32),

time: 68.1 us -> 45.4 us (0.67)
  the two profiles are of different devices: /device:TPU:1 before, /device:TPU:0 now
where the time goes in v2:
time: 45.4 us; the launch traced here: 45.2 us
  Pallas kernels  41.6 us (92%)
  local copies, waits for them, and re-layouts  2.98 us (7%)
  between operations  0.65 us (1%)
    pallas_call x1, Pallas kernels, local(): pl.pallas_call(functools.partial(kernel, n_lat, n_lon), out_shape=(jax.Sh...  41.6 us
    unnamed x4, local copies, waits for them, and re-layouts  2.98 us

profile of v2, /device:TPU:0, one launch (start us, length us, event | category | flops | bytes accessed | tf_op | source)
XLA Modules:
  0.0 45.2 jit_solution(13858574564176032825)
XLA Ops:
  0.6 41.6 %shard_map.59 = (bf16[32,128,128]{2,1,0:T(8,128)(2,1)}, f32[5,32,32]{2,1,0:T(8,128)}) custom-call(bf16[32,128,128]{2,1,0:T(8,128)(2,1)} %feat_hbm.1, bf16[32,128,128]{2,1,0:T(8,128)(2,1)} %cot_hbm.1, s32[128,128]{1,0:T(8,128)} %mask_hbm.1, bf16[5,32,32]{2,1,0:T(8,128)(2,1)} %w_hbm.1), custom_call_target="tpu_custom_call" | custom-call | tf_op jit(solution)/shard_map/pallas_call | solution.py:490
  42.2 0.0 copy-start
  42.2 2.3 %copy.8 = bf16[32,128,128]{2,1,0:T(8,128)(2,1)} copy(bf16[32,128,128]{2,1,0:T(8,128)(2,1)} %get-tuple-element.4) | data formatting | bytes 2097152
  44.6 0.0 copy-done
  44.6 0.6 %copy.9 = f32[5,32,32]{2,1,0:T(8,128)} copy(f32[5,32,32]{2,1,0:T(8,128)S(1)} %copy-done) | data formatting | bytes 40960
Async XLA Ops:
  42.2 2.4 %copy-start = (f32[5,32,32]{2,1,0:T(8,128)S(1)}, f32[5,32,32]{2,1,0:T(8,128)}, u32[]{:S(2)}) copy-start(f32[5,32,32]{2,1,0:T(8,128)} %get-tuple-element.5) | copy-start | bytes 61444

commit v3 on v2

--- a/solution.py
+++ b/solution.py
@@ -29,8 +29,8 @@
     out_hbm, wg_ref,
     feat_v, cot_v, mask_v, w_v, xf, cf, out_v,
     ya, yb, coef, scale, terms, gcat,
-    mb, sm, vm, snat, wf, wb, sel,
-    pack, lrow, lcol, own, ar1, ar2,
+    mtx, mrx, sm, vm, snat, wf, wb, sel,
+    pack, cpack, lrow, lcol, own, ar1, ar2,
     in_sem, out_sem, mask_send, mask_recv, halo_send, halo_recv,
     ar1_send, ar1_recv, ar2_send, ar2_recv,
 ):
@@ -80,7 +80,12 @@
     sel[...] = (inside | left | right).astype(F32).astype(BF16)
 
     mask_in.wait()
-    mb[1, 8 : 8 + B, :] = mask_v[...].astype(F32)
+    flags = mask_v[...].astype(F32)
+    turned_flags = flags.T
+    mtx[0] = flags[B - 8 :]
+    mtx[1] = flags[:8]
+    mtx[2] = turned_flags[B - 8 :]
+    mtx[3] = turned_flags[:8]
     pl.semaphore_wait(barrier, 4 + (n_lon - 1) + (n_lat - 1))
 
     def remote(src, dst, send, recv, i, j):
@@ -89,28 +94,28 @@
             device_id=(i, j), device_id_type=pl.DeviceIdType.MESH,
         )
 
-    mid, top, bottom = pl.ds(8, B), pl.ds(8, 8), pl.ds(B, 8)
+    mid = pl.ds(8, B)
     above, below = pl.ds(0, 8), pl.ds(8 + B, 8)
     mask_plan = (
-        (mid, 0, mid, lat, east),
-        (mid, 2, mid, lat, west),
-        (bottom, 1, above, south, lon),
-        (top, 1, below, north, lon),
-        (bottom, 0, above, south, east),
-        (bottom, 2, above, south, west),
-        (top, 0, below, north, east),
-        (top, 2, below, north, west),
+        (2, 0, lat, east),
+        (3, 1, lat, west),
+        (0, 2, south, lon),
+        (1, 3, north, lon),
+        (0, 4, south, east),
+        (0, 5, south, west),
+        (1, 6, north, east),
+        (1, 7, north, west),
     )
     mask_copies = [
-        remote(mb.at[1, src], mb.at[slot, dst], mask_send.at[n], mask_recv.at[n], i, j)
-        for n, (src, slot, dst, i, j) in enumerate(mask_plan)
+        remote(mtx.at[src], mrx.at[n], mask_send.at[n], mask_recv.at[n], i, j)
+        for src, n, i, j in mask_plan
     ]
     for copy in mask_copies:
         copy.start()
 
     lane = lax.broadcasted_iota(jnp.int32, (B, B), 1)
 
-    def halo_copies(phase, y):
+    def halo_copies(phase):
         plan = (
             (pack.at[phase, 0], lrow.at[phase, 0, mid], south, lon),
             (pack.at[phase, 1], lrow.at[phase, 1, mid], north, lon),
@@ -118,8 +123,10 @@
             (pack.at[phase, 0, pl.ds(0, 8)], lrow.at[phase, 0, below], south, west),
             (pack.at[phase, 1, pl.ds(B - 8, 8)], lrow.at[phase, 1, above], north, east),
             (pack.at[phase, 1, pl.ds(0, 8)], lrow.at[phase, 1, below], north, west),
-            (y.at[pl.ds(H, R), pl.ds(O + B - 8, 8)], lcol.at[phase, 0], lat, east),
-            (y.at[pl.ds(H, R), pl.ds(O, 8)], lcol.at[phase, 1], lat, west),
+        ) + tuple(
+            (cpack.at[phase, side, at], lcol.at[phase, side, at], lat, (east, west)[side])
+            for at in (pl.ds(0, 2), pl.ds(14, 2), pl.ds(2, 4), pl.ds(6, 4), pl.ds(10, 4))
+            for side in range(2)
         )
         return [
             remote(src, dst, halo_send.at[phase, n], halo_recv.at[phase, n], i, j)
@@ -137,6 +144,29 @@
         pack[phase, 0] = last
         pack[phase, 1] = first
 
+    half = lax.broadcasted_iota(jnp.int32, (8, B), 0) < 4
+
+    def pack_columns(phase, y, p):
+        a, b = y[H + 2 * p, O + B - 8 : O + B, :], y[H + 2 * p + 1, O + B - 8 : O + B, :]
+        cpack[phase, 0, p] = jnp.where(half, pltpu.roll(a, 4, 0), b)
+        a, b = y[H + 2 * p, O : O + 8, :], y[H + 2 * p + 1, O : O + 8, :]
+        cpack[phase, 1, p] = jnp.where(half, a, pltpu.roll(b, 4, 0))
+
+    def send_chunks(phase, y, copies, turn_rows):
+        turn_rows(0, H)
+        turn_rows(R - H, H)
+        for p in (0, 1, 14, 15):
+            pack_columns(phase, y, p)
+        pack_rows(phase, y)
+        for copy in copies[:10]:
+            copy.start()
+        for n in range(3):
+            turn_rows(H + 8 * n, 8)
+            for p in range(2 + 4 * n, 6 + 4 * n):
+                pack_columns(phase, y, p)
+            for copy in copies[10 + 2 * n : 12 + 2 * n]:
+                copy.start()
+
     feat_in.wait()
 
     def widen(src, dst):
@@ -156,22 +186,12 @@
     def turn(r):
         yb[H + r, O : O + B, :] = rows_of(xf, r).T
 
-    def turn_edge(i, _):
-        turn(i + (R - 2 * H) * (i // H))
-        return 0
-
-    def turn_inner(i, _):
-        turn(i)
-        return 0
-
-    lax.fori_loop(0, 2 * H, turn_edge, 0, unroll=8)
-    first_halo = halo_copies(0, yb)
-    pack_rows(0, yb)
-    for copy in first_halo[:6]:
-        copy.start()
-    lax.fori_loop(H, R - H, turn_inner, 0, unroll=8)
-    for copy in first_halo[6:]:
-        copy.start()
+    def turn_rows(first, count):
+        for r in range(first, first + count):
+            turn(r)
+
+    first_halo = halo_copies(0)
+    send_chunks(0, yb, first_halo, turn_rows)
 
     w_in.wait()
     block = (row_i // C) == (col_i // C)
@@ -187,11 +207,17 @@
     north_ok = (lat > 0).astype(F32)
     south_ok = (lat < n_lat - 1).astype(F32)
     lane_e = lax.broadcasted_iota(jnp.int32, (CE, B), 1)
-    row_e = lax.broadcasted_iota(jnp.int32, (CE, B), 0)
-    ok = jnp.where(row_e < 8, north_ok, jnp.where(row_e >= 8 + B, south_ok, 1.0))
-    sm[...] = jnp.zeros_like(sm)
-    sm[0, 8 : 8 + CE, :] = mb[1] * ok
-    sm[1, 8 : 8 + CE, :] = jnp.where(lane_e < 64, mb[2], mb[0]) * ok
+    sm[:, 0:8, :] = jnp.zeros((2, 8, B), F32)
+    sm[:, 8 + CE :, :] = jnp.zeros((2, 8, B), F32)
+    sm[0, 8:16, :] = mrx[2] * north_ok
+    sm[0, 16 : 16 + B, :] = mask_v[...].astype(F32)
+    sm[0, 16 + B : 24 + B, :] = mrx[3] * south_ok
+    low_lanes = lane_e[0:8] < 64
+    sm[1, 8:16, :] = jnp.where(low_lanes, mrx[5], mrx[4]) * north_ok
+    sm[1, 16 : 16 + B, :] = jnp.concatenate(
+        [mrx[1], jnp.zeros((B - 16, B), F32), mrx[0]], axis=0
+    ).T
+    sm[1, 16 + B : 24 + B, :] = jnp.where(low_lanes, mrx[7], mrx[6]) * south_ok
 
     def ring(main, side, shift, edge):
         m, s = pltpu.roll(main, shift, 1), pltpu.roll(side, shift, 1)
@@ -230,12 +256,12 @@
     lax.fori_loop(0, RE // 2, spread, 0, unroll=4)
 
     def assemble(phase, y, ok_north, ok_south):
-        def sides(r, _):
-            y[H + r, O - 8 : O, :] = lcol[phase, 0, r]
-            y[H + r, O + B : O + B + 8, :] = lcol[phase, 1, r]
-            return 0
-
-        lax.fori_loop(0, R, sides, 0, unroll=4)
+        for p in range(R // 2):
+            a, b = lcol[phase, 0, p], lcol[phase, 1, p]
+            y[H + 2 * p, O - 8 : O, :] = pltpu.roll(a, 4, 0)
+            y[H + 2 * p + 1, O - 8 : O, :] = a
+            y[H + 2 * p, O + B : O + B + 8, :] = b
+            y[H + 2 * p + 1, O + B : O + B + 8, :] = pltpu.roll(b, 4, 0)
         for i in range(H):
             own_up = pltpu.roll(y[R + i, O - 8 : O + B + 8, :], 32, 1)
             far_up = pltpu.roll(lrow[phase, 0], (B - 32 * i) % B, 1) * ok_north
@@ -336,32 +362,14 @@
         w = -0.5 * coef[H + r, 8 : 8 + B, :] * scale[H + r, 8 : 8 + B, :]
         ya[H + r, O : O + B, :] = w * grad.T
 
-    def mix_edge(i, _):
-        mix(i + (R // 2 - H) * (i // (H // 2)))
-        return 0
-
-    def mix_inner(i, _):
-        mix(i)
-        return 0
-
-    def grad_edge(i, _):
-        turn_grad(i + (R - 2 * H) * (i // H))
-        return 0
-
-    def grad_inner(i, _):
-        turn_grad(i)
-        return 0
-
-    lax.fori_loop(0, H, mix_edge, 0, unroll=H)
-    lax.fori_loop(0, 2 * H, grad_edge, 0, unroll=8)
-    second_halo = halo_copies(1, ya)
-    pack_rows(1, ya)
-    for copy in second_halo[:6]:
-        copy.start()
-    lax.fori_loop(H // 2, R // 2 - H // 2, mix_inner, 0, unroll=4)
-    lax.fori_loop(H, R - H, grad_inner, 0, unroll=8)
-    for copy in second_halo[6:]:
-        copy.start()
+    def grad_rows(first, count):
+        for p in range(first // 2, (first + count) // 2):
+            mix(p)
+        for r in range(first, first + count):
+            turn_grad(r)
+
+    second_halo = halo_copies(1)
+    send_chunks(1, ya, second_halo, grad_rows)
 
     chunk = 8 * B
     acc = None
@@ -509,7 +517,8 @@
                 pltpu.VMEM((RE, CE, B), F32),
                 pltpu.VMEM((R * B, (K + 1) * B), BF16),
                 pltpu.VMEM((B, R * B), BF16),
-                pltpu.VMEM((3, CE, B), F32),
+                pltpu.VMEM((4, 8, B), F32),
+                pltpu.VMEM((8, 8, B), F32),
                 pltpu.VMEM((2, CP, B), F32),
                 pltpu.VMEM((CE, 2 * B), F32),
                 pltpu.VMEM((B, B), F32),
@@ -517,12 +526,13 @@
                 pltpu.VMEM((B, (K + 1) * B), BF16),
                 pltpu.VMEM((CE, 2 * B), BF16),
                 pltpu.VMEM((2, 2, B, B), F32),
+                pltpu.VMEM((2, 2, R // 2, 8, B), F32),
                 pltpu.VMEM((2, 2, CE, B), F32),
-                pltpu.VMEM((2, 2, R, 8, B), F32),
+                pltpu.VMEM((2, 2, R // 2, 8, B), F32),
                 pltpu.VMEM((2, C + 8, B), F32),
                 pltpu.VMEM((n_lon, C + 8, B), F32),
                 pltpu.VMEM((n_lat, C + 8, B), F32),
-                sem((4,)), sem(()), sem((8,)), sem((8,)), sem((2, 8)), sem((2, 8)),
+                sem((4,)), sem(()), sem((8,)), sem((8,)), sem((2, 16)), sem((2, 16)),
                 sem((n_lon,)), sem((n_lon,)), sem((n_lat,)), sem((n_lat,)),
             ],
             compiler_params=pltpu.CompilerParams(

time: 45.4 us -> 43 us (0.947)
  the two profiles are of different devices: /device:TPU:0 before, /device:TPU:1 now
where the time goes in v3:
time: 43 us; the launch traced here: 42.9 us
  Pallas kernels  39.3 us (91%)
  local copies, waits for them, and re-layouts  2.98 us (7%)
  between operations  0.65 us (2%)
    pallas_call x1, Pallas kernels, local(): pl.pallas_call(functools.partial(kernel, n_lat, n_lon), out_shape=(jax.Sh...  39.3 us
    unnamed x4, local copies, waits for them, and re-layouts  2.98 us

profile of v3, /device:TPU:1, one launch (start us, length us, event | category | flops | bytes accessed | tf_op | source)
XLA Modules:
  0.0 42.9 jit_solution(2058210177065801689)
XLA Ops:
  0.6 39.3 %shard_map.59 = (bf16[32,128,128]{2,1,0:T(8,128)(2,1)}, f32[5,32,32]{2,1,0:T(8,128)}) custom-call(bf16[32,128,128]{2,1,0:T(8,128)(2,1)} %feat_hbm.1, bf16[32,128,128]{2,1,0:T(8,128)(2,1)} %cot_hbm.1, s32[128,128]{1,0:T(8,128)} %mask_hbm.1, bf16[5,32,32]{2,1,0:T(8,128)(2,1)} %w_hbm.1), custom_call_target="tpu_custom_call" | custom-call | tf_op jit(solution)/shard_map/pallas_call | solution.py:498
  39.9 0.0 copy-start
  39.9 2.3 %copy.8 = bf16[32,128,128]{2,1,0:T(8,128)(2,1)} copy(bf16[32,128,128]{2,1,0:T(8,128)(2,1)} %get-tuple-element.4) | data formatting | bytes 2097152
  42.2 0.0 copy-done
  42.2 0.6 %copy.9 = f32[5,32,32]{2,1,0:T(8,128)} copy(f32[5,32,32]{2,1,0:T(8,128)S(1)} %copy-done) | data formatting | bytes 40960
Async XLA Ops:
  39.9 2.4 %copy-start = (f32[5,32,32]{2,1,0:T(8,128)S(1)}, f32[5,32,32]{2,1,0:T(8,128)}, u32[]{:S(2)}) copy-start(f32[5,32,32]{2,1,0:T(8,128)} %get-tuple-element.5) | copy-start | bytes 61444

commit v4 on v3

--- a/solution.py
+++ b/solution.py
@@ -26,12 +26,12 @@
 def kernel(
     n_lat, n_lon,
     feat_hbm, cot_hbm, mask_hbm, w_hbm,
-    out_hbm, wg_ref,
-    feat_v, cot_v, mask_v, w_v, xf, cf, out_v,
-    ya, yb, coef, scale, terms, gcat,
-    mtx, mrx, sm, vm, snat, wf, wb, sel,
+    terms, snat, wb, sum_ref,
+    feat_v, cot_v, mask_v, w_v, xf, cf,
+    ya, yb, coef, scale, gcat,
+    mtx, mrx, sm, vm, wf, sel,
     pack, cpack, lrow, lcol, own, ar1, ar2,
-    in_sem, out_sem, mask_send, mask_recv, halo_send, halo_recv,
+    in_sem, mask_send, mask_recv, halo_send, halo_recv,
     ar1_send, ar1_recv, ar2_send, ar2_recv,
 ):
     lat = lax.axis_index("lat")
@@ -440,7 +440,6 @@
 
     lax.fori_loop(0, R, keep_grad, 0, unroll=4)
     step(ya, yb, 1, False)
-    step(yb, ya, 2, False)
 
     run(n_lon, lambda off: lon_wait(off).wait())
     total = ar1[0]
@@ -450,9 +449,18 @@
     run(n_lat, lambda off: lat_copy(off).start())
     ar2[lat] = total
 
+    step(yb, ya, 2, False)
     step(ya, yb, 3, False)
     step(yb, ya, 4, False)
 
+    run(n_lat, lambda off: lat_wait(off).wait())
+    total = ar2[0]
+    for q in range(1, n_lat):
+        total = total + ar2[q]
+    sum_ref[...] = total
+
+
+def close(terms, snat, wb, sum_ref, out_hbm, wg_ref, xf, out_v, out_sem):
     def finish(p, _):
         t = terms[pl.ds(pl.multiple_of(2 * p * B, 2 * B), 2 * B), :]
         res = lax.dot_general(wb[...], t, NT, preferred_element_type=F32)
@@ -466,18 +474,18 @@
 
     lax.fori_loop(0, R // 2, finish, 0, unroll=4)
 
-    def narrow(c, _):
-        out_v[c] = xf[pl.ds(pl.multiple_of(c * B, B), B), :].astype(BF16)
-        return 0
-
-    lax.fori_loop(0, C, narrow, 0, unroll=4)
-    out_copy = pltpu.make_async_copy(out_v, out_hbm, out_sem)
-    out_copy.start()
-
-    run(n_lat, lambda off: lat_wait(off).wait())
-    total = ar2[0]
-    for q in range(1, n_lat):
-        total = total + ar2[q]
+    part = C // 4
+    copies = [
+        pltpu.make_async_copy(
+            out_v.at[pl.ds(n * part, part)], out_hbm.at[pl.ds(n * part, part)], out_sem.at[n]
+        )
+        for n in range(4)
+    ]
+    for n in range(4):
+        for c in range(n * part, (n + 1) * part):
+            out_v[c] = xf[c * B : (c + 1) * B, :].astype(BF16)
+        copies[n].start()
+    total = sum_ref[...]
     flat = total[0:C].T
     for k in range(K):
         wg_ref[k] = flat[k * C : (k + 1) * C, :]
@@ -486,23 +494,28 @@
         [last if g == 0 else pltpu.roll(last, B - C * g, 1) for g in range(RG)], axis=0
     )
     wg_ref[K] = last.T[0:C, :]
-    out_copy.wait()
+    for copy in copies:
+        copy.wait()
 
 
 def solution(mesh):
     n_lat, n_lon = mesh.shape["lat"], mesh.shape["lon"]
-    hbm = pl.BlockSpec(memory_space=pl.ANY)
+    hbm = pl.BlockSpec(memory_space=pltpu.HBM)
     sem = pltpu.SemaphoreType.DMA
 
     def local(features, cotangent, sea_mask, weights):
-        return pl.pallas_call(
+        vmem = pl.BlockSpec(memory_space=pltpu.VMEM)
+        carried = (
+            pltpu.VMEM((R * B, (K + 1) * B), BF16),
+            pltpu.VMEM((B, B), F32),
+            pltpu.VMEM((B, (K + 1) * B), BF16),
+            pltpu.VMEM((C + 8, B), F32),
+        )
+        carried = pl.pallas_call(
             functools.partial(kernel, n_lat, n_lon),
-            out_shape=(
-                jax.ShapeDtypeStruct((C, B, B), BF16),
-                jax.ShapeDtypeStruct((K + 1, C, C), F32),
-            ),
+            out_shape=carried,
             in_specs=[hbm] * 4,
-            out_specs=(hbm, pl.BlockSpec(memory_space=pltpu.VMEM)),
+            out_specs=(vmem,) * 4,
             scratch_shapes=[
                 pltpu.VMEM((C, B, B), BF16),
                 pltpu.VMEM((C, B, B), BF16),
@@ -510,19 +523,15 @@
                 pltpu.VMEM((K + 1, C, C), BF16),
                 pltpu.VMEM((C * B, B), F32),
                 pltpu.VMEM((C * B, B), F32),
-                pltpu.VMEM((C, B, B), BF16),
                 pltpu.VMEM((RE, CP, B), F32),
                 pltpu.VMEM((RE, CP, B), F32),
                 pltpu.VMEM((RE, CE, B), F32),
                 pltpu.VMEM((RE, CE, B), F32),
-                pltpu.VMEM((R * B, (K + 1) * B), BF16),
                 pltpu.VMEM((B, R * B), BF16),
                 pltpu.VMEM((4, 8, B), F32),
                 pltpu.VMEM((8, 8, B), F32),
                 pltpu.VMEM((2, CP, B), F32),
                 pltpu.VMEM((CE, 2 * B), F32),
-                pltpu.VMEM((B, B), F32),
-                pltpu.VMEM((B, (K + 1) * B), BF16),
                 pltpu.VMEM((B, (K + 1) * B), BF16),
                 pltpu.VMEM((CE, 2 * B), BF16),
                 pltpu.VMEM((2, 2, B, B), F32),
@@ -532,13 +541,24 @@
                 pltpu.VMEM((2, C + 8, B), F32),
                 pltpu.VMEM((n_lon, C + 8, B), F32),
                 pltpu.VMEM((n_lat, C + 8, B), F32),
-                sem((4,)), sem(()), sem((8,)), sem((8,)), sem((2, 16)), sem((2, 16)),
+                sem((4,)), sem((8,)), sem((8,)), sem((2, 16)), sem((2, 16)),
                 sem((n_lon,)), sem((n_lon,)), sem((n_lat,)), sem((n_lat,)),
             ],
             compiler_params=pltpu.CompilerParams(
-                collective_id=0, has_side_effects=True, vmem_limit_bytes=56 << 20
+                collective_id=0, has_side_effects=True, vmem_limit_bytes=40 << 20
             ),
         )(features, cotangent, sea_mask, weights)
+        return pl.pallas_call(
+            close,
+            out_shape=(
+                jax.ShapeDtypeStruct((C, B, B), BF16),
+                jax.ShapeDtypeStruct((K + 1, C, C), F32),
+            ),
+            in_specs=[vmem] * 4,
+            out_specs=(hbm, vmem),
+            scratch_shapes=[pltpu.VMEM((C * B, B), F32), pltpu.VMEM((C, B, B), BF16), sem((4,))],
+            compiler_params=pltpu.CompilerParams(vmem_limit_bytes=16 << 20),
+        )(*carried)
 
     placed = (P(None, "lat", "lon"), P(None, "lat", "lon"), P("lat", "lon"), P())
     return jax.shard_map(

time: 43 us -> 45.8 us (1.065); the launches traced: 42.9 us -> 45.2 us
  Pallas kernels: 39.3 us -> 40.5 us
  local copies, waits for them, and re-layouts: 2.98 us -> 4.06 us
    pallas_call x1 -> x2, Pallas kernels: 39.3 us -> 40.5 us  [the longest x1 35.6 us: local(): pl.pallas_call(functools.partial(kernel, n_lat, n_lon), out_shape=carried...]
    unnamed x4 -> x8, local copies, waits for them, and re-layouts: 2.98 us -> 4.06 us
where the time goes in v4:
time: 45.8 us; the launch traced here: 45.2 us
  Pallas kernels  40.5 us (88%)
  local copies, waits for them, and re-layouts  4.06 us (9%)
  between operations  0.65 us (1%)
    pallas_call x1, Pallas kernels, local(): pl.pallas_call(functools.partial(kernel, n_lat, n_lon), out_shape=carried...  35.6 us
    pallas_call x1, Pallas kernels, local(): pl.pallas_call(close, out_shape=(jax.ShapeDtypeStruct((C, B, B), BF16), j...  4.86 us
    unnamed x8, local copies, waits for them, and re-layouts  4.06 us

profile of v4, /device:TPU:1, one launch (start us, length us, event | category | flops | bytes accessed | tf_op | source)
XLA Modules:
  0.0 45.2 jit_solution(3516501878633986109)
XLA Ops:
  0.6 0.0 copy-start
  0.6 1.2 %copy-done = bf16[32,128,128]{2,1,0:T(8,128)(2,1)S(1)} copy-done((bf16[32,128,128]{2,1,0:T(8,128)(2,1)S(1)}, bf16[32,128,128]{2,1,0:T(8,128)(2,1)}, u32[]{:S(2)}) %copy-start) | copy-done | bytes 1048600
  1.9 0.0 copy-start.1
  1.9 1.2 %copy-done.1 = bf16[32,128,128]{2,1,0:T(8,128)(2,1)S(1)} copy-done((bf16[32,128,128]{2,1,0:T(8,128)(2,1)S(1)}, bf16[32,128,128]{2,1,0:T(8,128)(2,1)}, u32[]{:S(2)}) %copy-start.1) | copy-done | bytes 1048600
  3.1 0.0 copy-start.2
  3.1 0.8 %copy-done.2 = s32[128,128]{1,0:T(8,128)S(1)} copy-done((s32[128,128]{1,0:T(8,128)S(1)}, s32[128,128]{1,0:T(8,128)}, u32[]{:S(2)}) %copy-start.2) | copy-done | bytes 65560
  3.9 0.0 copy-start.3
  3.9 0.8 %copy-done.3 = bf16[5,32,32]{2,1,0:T(8,128)(2,1)S(1)} copy-done((bf16[5,32,32]{2,1,0:T(8,128)(2,1)S(1)}, bf16[5,32,32]{2,1,0:T(8,128)(2,1)}, u32[]{:S(2)}) %copy-start.3) | copy-done | bytes 10264
  4.7 35.6 %shard_map.59 = (bf16[4096,640]{1,0:T(8,128)(2,1)S(1)}, f32[128,128]{1,0:T(8,128)S(1)}, bf16[128,640]{1,0:T(8,128)(2,1)S(1)}, f32[40,128]{1,0:T(8,128)S(1)}) custom-call(bf16[32,128,128]{2,1,0:T(8,128)(2,1)S(1)} %copy-done, bf16[32,128,128]{2,1,0:T(8,128)(2,1)S(1)} %copy-done.1, s32[128,128]{1,0:T(8,128)S(1)} %copy-done.2, bf16[5,32,32]{2,1,0:T(8,128)(2,1)S(1)} %copy-done.3), custom_call_target="tpu_custom_call" | custom-call | tf_op jit(solution)/shard_map/pallas_call | solution.py:514
  40.3 4.9 %shard_map.60 = (bf16[32,128,128]{2,1,0:T(8,128)(2,1)}, f32[5,32,32]{2,1,0:T(8,128)}) custom-call(bf16[4096,640]{1,0:T(8,128)(2,1)S(1)} %get-tuple-element.6.terms, f32[128,128]{1,0:T(8,128)S(1)} %get-tuple-element.7.snat, bf16[128,640]{1,0:T(8,128)(2,1)S(1)} %get-tuple-element.8.wb, f32[40,128]{1,0:T(8,128)S(1)} %get-tuple-element.9.sum_ref), custom_call_target="tpu_custom_call" | custom-call | tf_op jit(solution)/shard_map/pallas_call | solution.py:551
Async XLA Ops:
  0.6 1.2 %copy-start = (bf16[32,128,128]{2,1,0:T(8,128)(2,1)S(1)}, bf16[32,128,128]{2,1,0:T(8,128)(2,1)}, u32[]{:S(2)}) copy-start(bf16[32,128,128]{2,1,0:T(8,128)(2,1)} %feat_hbm.1) | copy-start | bytes 3145732
  1.9 1.2 %copy-start.1 = (bf16[32,128,128]{2,1,0:T(8,128)(2,1)S(1)}, bf16[32,128,128]{2,1,0:T(8,128)(2,1)}, u32[]{:S(2)}) copy-start(bf16[32,128,128]{2,1,0:T(8,128)(2,1)} %cot_hbm.1) | copy-start | bytes 3145732
  3.1 0.8 %copy-start.2 = (s32[128,128]{1,0:T(8,128)S(1)}, s32[128,128]{1,0:T(8,128)}, u32[]{:S(2)}) copy-start(s32[128,128]{1,0:T(8,128)} %mask_hbm.1) | copy-start | bytes 196612
  3.9 0.8 %copy-start.3 = (bf16[5,32,32]{2,1,0:T(8,128)(2,1)S(1)}, bf16[5,32,32]{2,1,0:T(8,128)(2,1)}, u32[]{:S(2)}) copy-start(bf16[5,32,32]{2,1,0:T(8,128)(2,1)} %w_hbm.1) | copy-start | bytes 30724

commit v5 on v4

--- a/solution.py
+++ b/solution.py
@@ -545,7 +545,7 @@
                 sem((n_lon,)), sem((n_lon,)), sem((n_lat,)), sem((n_lat,)),
             ],
             compiler_params=pltpu.CompilerParams(
-                collective_id=0, has_side_effects=True, vmem_limit_bytes=40 << 20
+                collective_id=0, has_side_effects=True, vmem_limit_bytes=58 << 20
             ),
         )(features, cotangent, sea_mask, weights)
         return pl.pallas_call(

time: 45.8 us -> 41.3 us (0.902)
  local copies, waits for them, and re-layouts: 4.06 us -> 0 us
    unnamed x8 -> x0, local copies, waits for them, and re-layouts: 4.06 us -> none
where the time goes in v5:
time: 41.3 us; the launch traced here: 40.9 us
  Pallas kernels  40.3 us (98%)
  between operations  0.64 us (2%)
    pallas_call x1, Pallas kernels, local(): pl.pallas_call(functools.partial(kernel, n_lat, n_lon), out_shape=carried...  35.4 us
    pallas_call x1, Pallas kernels, local(): pl.pallas_call(close, out_shape=(jax.ShapeDtypeStruct((C, B, B), BF16), j...  4.87 us

profile of v5, /device:TPU:1, one launch (start us, length us, event | category | flops | bytes accessed | tf_op | source)
XLA Modules:
  0.0 40.9 jit_solution(16575260739195282573)
XLA Ops:
  0.6 35.4 %shard_map.59 = (bf16[4096,640]{1,0:T(8,128)(2,1)S(1)}, f32[128,128]{1,0:T(8,128)S(1)}, bf16[128,640]{1,0:T(8,128)(2,1)S(1)}, f32[40,128]{1,0:T(8,128)S(1)}) custom-call(bf16[32,128,128]{2,1,0:T(8,128)(2,1)} %feat_hbm.1, bf16[32,128,128]{2,1,0:T(8,128)(2,1)} %cot_hbm.1, s32[128,128]{1,0:T(8,128)} %mask_hbm.1, bf16[5,32,32]{2,1,0:T(8,128)(2,1)} %w_hbm.1), custom_call_target="tpu_custom_call" | custom-call | tf_op jit(solution)/shard_map/pallas_call | solution.py:514
  36.1 4.9 %shard_map.60 = (bf16[32,128,128]{2,1,0:T(8,128)(2,1)}, f32[5,32,32]{2,1,0:T(8,128)}) custom-call(bf16[4096,640]{1,0:T(8,128)(2,1)S(1)} %get-tuple-element.6.terms, f32[128,128]{1,0:T(8,128)S(1)} %get-tuple-element.7.snat, bf16[128,640]{1,0:T(8,128)(2,1)S(1)} %get-tuple-element.8.wb, f32[40,128]{1,0:T(8,128)S(1)} %get-tuple-element.9.sum_ref), custom_call_target="tpu_custom_call" | custom-call | tf_op jit(solution)/shard_map/pallas_call | solution.py:551

commit v6 on v5

--- a/solution.py
+++ b/solution.py
@@ -26,10 +26,10 @@
 def kernel(
     n_lat, n_lon,
     feat_hbm, cot_hbm, mask_hbm, w_hbm,
-    terms, snat, wb, sum_ref,
+    out_v, sum_ref,
     feat_v, cot_v, mask_v, w_v, xf, cf,
-    ya, yb, coef, scale, gcat,
-    mtx, mrx, sm, vm, wf, sel,
+    ya, yb, coef, scale, terms, gcat,
+    mtx, mrx, sm, vm, snat, wf, wb, sel,
     pack, cpack, lrow, lcol, own, ar1, ar2,
     in_sem, mask_send, mask_recv, halo_send, halo_recv,
     ar1_send, ar1_recv, ar2_send, ar2_recv,
@@ -202,6 +202,9 @@
         wb[:, k * B : (k + 1) * B] = full.astype(BF16)
         wf[:, k * B : (k + 1) * B] = full.T.astype(BF16)
 
+    cot_in.wait()
+    widen(cot_v, cf)
+
     for copy in mask_copies:
         copy.wait()
     north_ok = (lat > 0).astype(F32)
@@ -347,8 +350,6 @@
     step(ya, yb, 3, True)
     step(yb, ya, 4, True)
 
-    cot_in.wait()
-    widen(cot_v, cf)
 
     def mix(p):
         at = pl.ds(pl.multiple_of(2 * p * B, 2 * B), 2 * B)
@@ -430,15 +431,15 @@
     run(n_lon, lambda off: lon_copy(off).start())
     ar1[lon] = own[0]
 
+    def keep_grad(r, _):
+        keep(0, r, ya[H + r, O : O + B, :])
+        return 0
+
+    lax.fori_loop(0, R, keep_grad, 0, unroll=4)
     for copy in second_halo:
         copy.wait()
     assemble(1, ya, north_ok, south_ok)
 
-    def keep_grad(r, _):
-        keep(0, r, ya[H + r, O : O + B, :])
-        return 0
-
-    lax.fori_loop(0, R, keep_grad, 0, unroll=4)
     step(ya, yb, 1, False)
 
     run(n_lon, lambda off: lon_wait(off).wait())
@@ -453,14 +454,6 @@
     step(ya, yb, 3, False)
     step(yb, ya, 4, False)
 
-    run(n_lat, lambda off: lat_wait(off).wait())
-    total = ar2[0]
-    for q in range(1, n_lat):
-        total = total + ar2[q]
-    sum_ref[...] = total
-
-
-def close(terms, snat, wb, sum_ref, out_hbm, wg_ref, xf, out_v, out_sem):
     def finish(p, _):
         t = terms[pl.ds(pl.multiple_of(2 * p * B, 2 * B), 2 * B), :]
         res = lax.dot_general(wb[...], t, NT, preferred_element_type=F32)
@@ -474,17 +467,19 @@
 
     lax.fori_loop(0, R // 2, finish, 0, unroll=4)
 
-    part = C // 4
-    copies = [
-        pltpu.make_async_copy(
-            out_v.at[pl.ds(n * part, part)], out_hbm.at[pl.ds(n * part, part)], out_sem.at[n]
-        )
-        for n in range(4)
-    ]
-    for n in range(4):
-        for c in range(n * part, (n + 1) * part):
-            out_v[c] = xf[c * B : (c + 1) * B, :].astype(BF16)
-        copies[n].start()
+    for c in range(C):
+        out_v[c] = xf[c * B : (c + 1) * B, :].astype(BF16)
+
+    run(n_lat, lambda off: lat_wait(off).wait())
+    total = ar2[0]
+    for q in range(1, n_lat):
+        total = total + ar2[q]
+    sum_ref[...] = total
+
+
+def close(out_v, sum_ref, out_hbm, wg_ref, out_sem):
+    copy = pltpu.make_async_copy(out_v, out_hbm, out_sem)
+    copy.start()
     total = sum_ref[...]
     flat = total[0:C].T
     for k in range(K):
@@ -494,8 +489,7 @@
         [last if g == 0 else pltpu.roll(last, B - C * g, 1) for g in range(RG)], axis=0
     )
     wg_ref[K] = last.T[0:C, :]
-    for copy in copies:
-        copy.wait()
+    copy.wait()
 
 
 def solution(mesh):
@@ -506,16 +500,14 @@
     def local(features, cotangent, sea_mask, weights):
         vmem = pl.BlockSpec(memory_space=pltpu.VMEM)
         carried = (
-            pltpu.VMEM((R * B, (K + 1) * B), BF16),
-            pltpu.VMEM((B, B), F32),
-            pltpu.VMEM((B, (K + 1) * B), BF16),
+            pltpu.VMEM((C, B, B), BF16),
             pltpu.VMEM((C + 8, B), F32),
         )
         carried = pl.pallas_call(
             functools.partial(kernel, n_lat, n_lon),
             out_shape=carried,
             in_specs=[hbm] * 4,
-            out_specs=(vmem,) * 4,
+            out_specs=(vmem,) * 2,
             scratch_shapes=[
                 pltpu.VMEM((C, B, B), BF16),
                 pltpu.VMEM((C, B, B), BF16),
@@ -527,11 +519,14 @@
                 pltpu.VMEM((RE, CP, B), F32),
                 pltpu.VMEM((RE, CE, B), F32),
                 pltpu.VMEM((RE, CE, B), F32),
+                pltpu.VMEM((R * B, (K + 1) * B), BF16),
                 pltpu.VMEM((B, R * B), BF16),
                 pltpu.VMEM((4, 8, B), F32),
                 pltpu.VMEM((8, 8, B), F32),
                 pltpu.VMEM((2, CP, B), F32),
                 pltpu.VMEM((CE, 2 * B), F32),
+                pltpu.VMEM((B, B), F32),
+                pltpu.VMEM((B, (K + 1) * B), BF16),
                 pltpu.VMEM((B, (K + 1) * B), BF16),
                 pltpu.VMEM((CE, 2 * B), BF16),
                 pltpu.VMEM((2, 2, B, B), F32),
@@ -545,7 +540,7 @@
                 sem((n_lon,)), sem((n_lon,)), sem((n_lat,)), sem((n_lat,)),
             ],
             compiler_params=pltpu.CompilerParams(
-                collective_id=0, has_side_effects=True, vmem_limit_bytes=58 << 20
+                collective_id=0, has_side_effects=True, vmem_limit_bytes=62 << 20
             ),
         )(features, cotangent, sea_mask, weights)
         return pl.pallas_call(
@@ -554,10 +549,10 @@
                 jax.ShapeDtypeStruct((C, B, B), BF16),
                 jax.ShapeDtypeStruct((K + 1, C, C), F32),
             ),
-            in_specs=[vmem] * 4,
+            in_specs=[vmem] * 2,
             out_specs=(hbm, vmem),
-            scratch_shapes=[pltpu.VMEM((C * B, B), F32), pltpu.VMEM((C, B, B), BF16), sem((4,))],
-            compiler_params=pltpu.CompilerParams(vmem_limit_bytes=16 << 20),
+            scratch_shapes=[sem(())],
+            compiler_params=pltpu.CompilerParams(vmem_limit_bytes=4 << 20),
         )(*carried)
 
     placed = (P(None, "lat", "lon"), P(None, "lat", "lon"), P("lat", "lon"), P())

time: 41.3 us -> 40.9 us (level)
    pallas_call x1, Pallas kernels: 4.87 us -> 1.61 us  [local(): pl.pallas_call(close, out_shape=(jax.ShapeDtypeStruct((C, B, B), BF16), j...]
    pallas_call x1, Pallas kernels: 35.4 us -> 38.5 us  [local(): pl.pallas_call(functools.partial(kernel, n_lat, n_lon), out_shape=carried...]
where the time goes in v6:
time: 40.9 us; the launch traced here: 40.8 us
  Pallas kernels  40.2 us (98%)
  between operations  0.64 us (2%)
    pallas_call x1, Pallas kernels, local(): pl.pallas_call(functools.partial(kernel, n_lat, n_lon), out_shape=carried...  38.5 us
    pallas_call x1, Pallas kernels, local(): pl.pallas_call(close, out_shape=(jax.ShapeDtypeStruct((C, B, B), BF16), j...  1.61 us

profile of v6, /device:TPU:1, one launch (start us, length us, event | category | flops | bytes accessed | tf_op | source)
XLA Modules:
  0.0 40.8 jit_solution(769119197802081893)
XLA Ops:
  0.6 38.5 %shard_map.59 = (bf16[32,128,128]{2,1,0:T(8,128)(2,1)S(1)}, f32[40,128]{1,0:T(8,128)S(1)}) custom-call(bf16[32,128,128]{2,1,0:T(8,128)(2,1)} %feat_hbm.1, bf16[32,128,128]{2,1,0:T(8,128)(2,1)} %cot_hbm.1, s32[128,128]{1,0:T(8,128)} %mask_hbm.1, bf16[5,32,32]{2,1,0:T(8,128)(2,1)} %w_hbm.1), custom_call_target="tpu_custom_call" | custom-call | tf_op jit(solution)/shard_map/pallas_call | solution.py:506
  39.2 1.6 %shard_map.60 = (bf16[32,128,128]{2,1,0:T(8,128)(2,1)}, f32[5,32,32]{2,1,0:T(8,128)}) custom-call(bf16[32,128,128]{2,1,0:T(8,128)(2,1)S(1)} %get-tuple-element.4.out_v, f32[40,128]{1,0:T(8,128)S(1)} %get-tuple-element.5.sum_ref), custom_call_target="tpu_custom_call" | custom-call | tf_op jit(solution)/shard_map/pallas_call | solution.py:546

commit v7 on v6

--- a/solution.py
+++ b/solution.py
@@ -258,6 +258,21 @@
 
     lax.fori_loop(0, RE // 2, spread, 0, unroll=4)
 
+    def groups(y):
+        for i in range(H):
+            y[i, O : O + B, :] = pltpu.roll(y[R + i, O : O + B, :], C, 1)
+            y[H + R + i, O : O + B, :] = pltpu.roll(y[H + i, O : O + B, :], B - C, 1)
+
+    def beside(y, at, row, shift):
+        return jnp.concatenate(
+            [
+                pltpu.roll(y[row, O - 8 : O, :], shift, 1),
+                y[at, O : O + B, :],
+                pltpu.roll(y[row, O + B : O + B + 8, :], shift, 1),
+            ],
+            axis=0,
+        )
+
     def assemble(phase, y, ok_north, ok_south):
         for p in range(R // 2):
             a, b = lcol[phase, 0, p], lcol[phase, 1, p]
@@ -266,10 +281,10 @@
             y[H + 2 * p, O + B : O + B + 8, :] = b
             y[H + 2 * p + 1, O + B : O + B + 8, :] = pltpu.roll(b, 4, 0)
         for i in range(H):
-            own_up = pltpu.roll(y[R + i, O - 8 : O + B + 8, :], 32, 1)
+            own_up = beside(y, i, R + i, C)
             far_up = pltpu.roll(lrow[phase, 0], (B - 32 * i) % B, 1) * ok_north
             y[i, O - 8 : O + B + 8, :] = jnp.where(lane_e < 32, far_up, own_up)
-            own_down = pltpu.roll(y[H + i, O - 8 : O + B + 8, :], B - 32, 1)
+            own_down = beside(y, H + R + i, H + i, B - C)
             far_down = pltpu.roll(lrow[phase, 1], (96 - 32 * i) % B, 1) * ok_south
             y[H + R + i, O - 8 : O + B + 8, :] = jnp.where(
                 lane_e >= 96, far_down, own_down
@@ -329,22 +344,86 @@
         if reach:
             lax.fori_loop(H + R, H + R + reach, outer, carried, unroll=reach)
 
+    def cells(src, dst, k, bands, rows, unroll):
+        def sums(r, first, size):
+            mid_ = src[r, first : first + size, :]
+            low = src[r, first - 1 : first - 1 + size, :]
+            high = src[r, first + 1 : first + 1 + size, :]
+            return mid_ + high, low + high, mid_ + low
+
+        def advance(r, carried, keeps):
+            after = []
+            for (first, size), (e0, e1, f1) in zip(bands, carried):
+                e2, f2, h2 = sums(r + 1, first, size)
+                total = coef[r, first - O + 8 : first - O + 8 + size, :] * (e0 + f1 + h2)
+                if k == 1:
+                    value = 0.5 * total
+                else:
+                    value = total - dst[r, first : first + size, :]
+                dst[r, first : first + size, :] = value
+                lo, hi = max(first, O), min(first + size, O + B)
+                if keeps:
+                    at = (r - H) * B + lo - O
+                    if not isinstance(r, int):
+                        at = pl.multiple_of(at, 8)
+                    terms[pl.ds(at, hi - lo), k * B : (k + 1) * B] = value[
+                        lo - first : hi - first
+                    ].astype(BF16)
+                after.append((e1, e2, f2))
+            return tuple(after)
+
+        low, high = rows
+        carried = tuple(
+            (sums(low - 1, *band)[0],) + sums(low, *band)[:2] for band in bands
+        )
+        if unroll:
+            lax.fori_loop(
+                low, high, lambda r, c: advance(r, c, True), carried, unroll=unroll
+            )
+        else:
+            for r in range(low, high):
+                carried = advance(r, carried, H <= r < H + R)
+
+    def step_inside(src, dst, k):
+        first, last = O + 8 * k, O + B - 8 * k
+        size = (last - first) // (1 if k == K else 2)
+        for at in range(first, last, size):
+            cells(src, dst, k, ((at, size),), (H + k, H + R - k), (0, 6, 7, 13, 8)[k])
+
+    def step_rim(src, dst, k):
+        reach = K - k
+        first, last = (O - 8, O + B + 8) if reach else (O, O + B)
+        size = 48 if reach else 64
+        for low in (H - reach, H + R - k):
+            for at in range(first, last, size):
+                cells(src, dst, k, ((at, size),), (low, low + K), 0)
+        width = O + 8 * k - first
+        bands = ((first, width), (last - width, width))
+        cells(src, dst, k, bands, (H + k, H + R - k), (0, 6, 7, 13, 8)[k])
+
     for copy in first_halo:
         copy.wait()
+    groups(yb)
     assemble(0, yb, 1.0, 1.0)
 
     def start_row(r, _):
         x = yb[r, O - 8 : O + B + 8, :]
-        ya[r, O - 8 : O + B + 8, :] = (-0.5 * coef[r] * scale[r]) * x
+        value = (-0.5 * coef[r] * scale[r]) * x
+        ya[r, O - 8 : O + B + 8, :] = value
+        return value
+
+    def start_halo(r, _):
+        start_row(r, 0)
         return 0
 
-    lax.fori_loop(0, RE, start_row, 0, unroll=4)
-
-    def keep_first(r, _):
-        keep(0, r, ya[H + r, O : O + B, :] * scale[H + r, 8 : 8 + B, :])
+    def start_own(r, _):
+        keep(0, r - H, start_row(r, 0)[8 : 8 + B] * scale[r, 8 : 8 + B, :])
         return 0
 
-    lax.fori_loop(0, R, keep_first, 0, unroll=4)
+    lax.fori_loop(0, H, start_halo, 0, unroll=4)
+    lax.fori_loop(H, H + R, start_own, 0, unroll=4)
+    lax.fori_loop(H + R, RE, start_halo, 0, unroll=4)
+
     step(ya, yb, 1, True)
     step(yb, ya, 2, True)
     step(ya, yb, 3, True)
@@ -436,11 +515,16 @@
         return 0
 
     lax.fori_loop(0, R, keep_grad, 0, unroll=4)
+    groups(ya)
+    step_inside(ya, yb, 1)
+    step_inside(yb, ya, 2)
+    step_inside(ya, yb, 3)
+    step_inside(yb, ya, 4)
     for copy in second_halo:
         copy.wait()
     assemble(1, ya, north_ok, south_ok)
 
-    step(ya, yb, 1, False)
+    step_rim(ya, yb, 1)
 
     run(n_lon, lambda off: lon_wait(off).wait())
     total = ar1[0]
@@ -450,9 +534,9 @@
     run(n_lat, lambda off: lat_copy(off).start())
     ar2[lat] = total
 
-    step(yb, ya, 2, False)
-    step(ya, yb, 3, False)
-    step(yb, ya, 4, False)
+    step_rim(yb, ya, 2)
+    step_rim(ya, yb, 3)
+    step_rim(yb, ya, 4)
 
     def finish(p, _):
         t = terms[pl.ds(pl.multiple_of(2 * p * B, 2 * B), 2 * B), :]

time: 40.9 us -> 39.4 us (0.963)
  Pallas kernels: 40.2 us -> 38.7 us
    pallas_call x1, Pallas kernels: 38.5 us -> 37 us  [local(): pl.pallas_call(functools.partial(kernel, n_lat, n_lon), out_shape=carried...]
where the time goes in v7:
time: 39.4 us; the launch traced here: 39.3 us
  Pallas kernels  38.7 us (98%)
  between operations  0.64 us (2%)
    pallas_call x1, Pallas kernels, local(): pl.pallas_call(functools.partial(kernel, n_lat, n_lon), out_shape=carried...  37 us
    pallas_call x1, Pallas kernels, local(): pl.pallas_call(close, out_shape=(jax.ShapeDtypeStruct((C, B, B), BF16), j...  1.61 us

profile of v7, /device:TPU:1, one launch (start us, length us, event | category | flops | bytes accessed | tf_op | source)
XLA Modules:
  0.0 39.3 jit_solution(11315327209125620527)
XLA Ops:
  0.6 37.0 %shard_map.59 = (bf16[32,128,128]{2,1,0:T(8,128)(2,1)S(1)}, f32[40,128]{1,0:T(8,128)S(1)}) custom-call(bf16[32,128,128]{2,1,0:T(8,128)(2,1)} %feat_hbm.1, bf16[32,128,128]{2,1,0:T(8,128)(2,1)} %cot_hbm.1, s32[128,128]{1,0:T(8,128)} %mask_hbm.1, bf16[5,32,32]{2,1,0:T(8,128)(2,1)} %w_hbm.1), custom_call_target="tpu_custom_call" | custom-call | tf_op jit(solution)/shard_map/pallas_call | solution.py:590
  37.7 1.6 %shard_map.60 = (bf16[32,128,128]{2,1,0:T(8,128)(2,1)}, f32[5,32,32]{2,1,0:T(8,128)}) custom-call(bf16[32,128,128]{2,1,0:T(8,128)(2,1)S(1)} %get-tuple-element.4.out_v, f32[40,128]{1,0:T(8,128)S(1)} %get-tuple-element.5.sum_ref), custom_call_target="tpu_custom_call" | custom-call | tf_op jit(solution)/shard_map/pallas_call | solution.py:630

commit v8 on v7

--- a/solution.py
+++ b/solution.py
@@ -205,40 +205,28 @@
     cot_in.wait()
     widen(cot_v, cf)
 
-    for copy in mask_copies:
-        copy.wait()
-    north_ok = (lat > 0).astype(F32)
-    south_ok = (lat < n_lat - 1).astype(F32)
     lane_e = lax.broadcasted_iota(jnp.int32, (CE, B), 1)
-    sm[:, 0:8, :] = jnp.zeros((2, 8, B), F32)
-    sm[:, 8 + CE :, :] = jnp.zeros((2, 8, B), F32)
-    sm[0, 8:16, :] = mrx[2] * north_ok
+    sm[...] = jnp.zeros_like(sm)
     sm[0, 16 : 16 + B, :] = mask_v[...].astype(F32)
-    sm[0, 16 + B : 24 + B, :] = mrx[3] * south_ok
-    low_lanes = lane_e[0:8] < 64
-    sm[1, 8:16, :] = jnp.where(low_lanes, mrx[5], mrx[4]) * north_ok
-    sm[1, 16 : 16 + B, :] = jnp.concatenate(
-        [mrx[1], jnp.zeros((B - 16, B), F32), mrx[0]], axis=0
-    ).T
-    sm[1, 16 + B : 24 + B, :] = jnp.where(low_lanes, mrx[7], mrx[6]) * south_ok
 
     def ring(main, side, shift, edge):
         m, s = pltpu.roll(main, shift, 1), pltpu.roll(side, shift, 1)
         at = lane_e == edge
         return jnp.where(at, s, m), jnp.where(at, m, s)
 
-    here = [sm[t, 8 : 8 + CE, :] for t in range(2)]
-    up = [sm[t, 7 : 7 + CE, :] for t in range(2)]
-    down = [sm[t, 9 : 9 + CE, :] for t in range(2)]
-    from_left = ring(here[0] + down[0], here[1] + down[1], 1, 0)
-    from_right = ring(here[0] + up[0], here[1] + up[1], B - 1, B - 1)
-    for t in range(2):
-        degree = from_left[t] + from_right[t] + up[t] + down[t]
-        vm[:, t * B : (t + 1) * B] = here[t] * jnp.maximum(degree, 1.0)
-        if t == 0:
-            snat[...] = jnp.sqrt(jnp.maximum(degree, 1.0)[8 : 8 + B])
-
-    def spread(p, _):
+    def degrees():
+        here = [sm[t, 8 : 8 + CE, :] for t in range(2)]
+        up = [sm[t, 7 : 7 + CE, :] for t in range(2)]
+        down = [sm[t, 9 : 9 + CE, :] for t in range(2)]
+        from_left = ring(here[0] + down[0], here[1] + down[1], 1, 0)
+        from_right = ring(here[0] + up[0], here[1] + up[1], B - 1, B - 1)
+        for t in range(2):
+            degree = from_left[t] + from_right[t] + up[t] + down[t]
+            vm[:, t * B : (t + 1) * B] = here[t] * jnp.maximum(degree, 1.0)
+            if t == 0:
+                snat[...] = jnp.sqrt(jnp.maximum(degree, 1.0)[8 : 8 + B])
+
+    def values(p, pick):
         rows = jnp.concatenate(
             [
                 jnp.broadcast_to(vm[pl.ds(8 - H + R * g + 2 * p + j, 1), :], (C, 2 * B))
@@ -247,16 +235,28 @@
             ],
             axis=0,
         )
-        v = lax.dot_general(sel[...], rows.astype(BF16), NT, preferred_element_type=F32)
+        v = lax.dot_general(pick, rows.astype(BF16), NT, preferred_element_type=F32)
         m = jnp.maximum(v, 1.0)
         rs = lax.rsqrt(m)
-        a, s = jnp.where(v > 0.5, -2.0 * rs * rs, 0.0), m * rs
+        return jnp.where(v > 0.5, -2.0 * rs * rs, 0.0), m * rs
+
+    def spread(p, _):
+        a, s = values(p, sel[...])
         for j in range(2):
             coef[2 * p + j] = a[:, j * B : (j + 1) * B]
             scale[2 * p + j] = s[:, j * B : (j + 1) * B]
         return 0
 
-    lax.fori_loop(0, RE // 2, spread, 0, unroll=4)
+    def spread_sides(p, _):
+        a, s = values(p, jnp.concatenate([sel[0:16, :], sel[CE - 16 :, :]], axis=0))
+        for j in range(2):
+            for ref, part in ((coef, a), (scale, s)):
+                ref[2 * p + j, 0:16, :] = part[0:16, j * B : (j + 1) * B]
+                ref[2 * p + j, CE - 16 :, :] = part[16:32, j * B : (j + 1) * B]
+        return 0
+
+    degrees()
+    lax.fori_loop(3, RE // 2 - 3, spread, 0, unroll=7)
 
     def groups(y):
         for i in range(H):
@@ -293,58 +293,7 @@
     def keep(k, r, value):
         terms[pl.ds(pl.multiple_of(r * B, B), B), k * B : (k + 1) * B] = value.astype(BF16)
 
-    def step(src, dst, k, scaled):
-        reach = K - k
-        first, count = (O - 8, CE) if reach else (O, B)
-        size = 48 if reach else 64
-        for at in range(0, count, size):
-            step_block(src, dst, k, scaled, first + at, size)
-
-    def step_block(src, dst, k, scaled, first, size):
-        reach = K - k
-        lo, hi = max(first, O), min(first + size, O + B)
-
-        def sums(r):
-            mid_ = src[r, first : first + size, :]
-            low = src[r, first - 1 : first - 1 + size, :]
-            high = src[r, first + 1 : first + 1 + size, :]
-            return mid_ + high, low + high, mid_ + low
-
-        def advance(r, carried):
-            e0, e1, f1 = carried
-            e2, f2, h2 = sums(r + 1)
-            a = coef[r, first - O + 8 : first - O + 8 + size, :]
-            total = a * (e0 + f1 + h2)
-            if k == 1:
-                value = 0.5 * total
-            else:
-                value = total - dst[r, first : first + size, :]
-            dst[r, first : first + size, :] = value
-            return (e1, e2, f2), value
-
-        def outer(r, carried):
-            return advance(r, carried)[0]
-
-        def inner(r, carried):
-            carried, value = advance(r, carried)
-            value = value[lo - first : hi - first]
-            if scaled:
-                value = value * scale[r, lo - O + 8 : hi - O + 8, :]
-            at = pl.multiple_of((r - H) * B + lo - O, 8)
-            terms[pl.ds(at, hi - lo), k * B : (k + 1) * B] = value.astype(BF16)
-            return carried
-
-        low = H - reach
-        e0 = sums(low - 1)[0]
-        e1, f1, _ = sums(low)
-        carried = (e0, e1, f1)
-        if reach:
-            carried = lax.fori_loop(low, H, outer, carried, unroll=reach)
-        carried = lax.fori_loop(H, H + R, inner, carried, unroll=8)
-        if reach:
-            lax.fori_loop(H + R, H + R + reach, outer, carried, unroll=reach)
-
-    def cells(src, dst, k, bands, rows, unroll):
+    def cells(src, dst, k, scaled, bands, rows, unroll):
         def sums(r, first, size):
             mid_ = src[r, first : first + size, :]
             low = src[r, first - 1 : first - 1 + size, :]
@@ -366,9 +315,10 @@
                     at = (r - H) * B + lo - O
                     if not isinstance(r, int):
                         at = pl.multiple_of(at, 8)
-                    terms[pl.ds(at, hi - lo), k * B : (k + 1) * B] = value[
-                        lo - first : hi - first
-                    ].astype(BF16)
+                    kept = value[lo - first : hi - first]
+                    if scaled:
+                        kept = kept * scale[r, lo - O + 8 : hi - O + 8, :]
+                    terms[pl.ds(at, hi - lo), k * B : (k + 1) * B] = kept.astype(BF16)
                 after.append((e1, e2, f2))
             return tuple(after)
 
@@ -384,50 +334,82 @@
             for r in range(low, high):
                 carried = advance(r, carried, H <= r < H + R)
 
-    def step_inside(src, dst, k):
+    def inner_rows(k, less):
+        low, high = H + k + less, H + R - k - less
+        return (low, high), {30: 6, 28: 7, 26: 13, 24: 8, 22: 11, 20: 10}[high - low]
+
+    def step_inside(src, dst, k, scaled, less):
         first, last = O + 8 * k, O + B - 8 * k
         size = (last - first) // (1 if k == K else 2)
         for at in range(first, last, size):
-            cells(src, dst, k, ((at, size),), (H + k, H + R - k), (0, 6, 7, 13, 8)[k])
-
-    def step_rim(src, dst, k):
+            cells(src, dst, k, scaled, ((at, size),), *inner_rows(k, less))
+
+    def step_rim(src, dst, k, scaled, less):
         reach = K - k
         first, last = (O - 8, O + B + 8) if reach else (O, O + B)
         size = 48 if reach else 64
-        for low in (H - reach, H + R - k):
+        for low in (H - reach, H + R - k - less):
             for at in range(first, last, size):
-                cells(src, dst, k, ((at, size),), (low, low + K), 0)
+                cells(src, dst, k, scaled, ((at, size),), (low, low + K + less), 0)
         width = O + 8 * k - first
         bands = ((first, width), (last - width, width))
-        cells(src, dst, k, bands, (H + k, H + R - k), (0, 6, 7, 13, 8)[k])
+        cells(src, dst, k, scaled, bands, *inner_rows(k, less))
+
+    def start_row(r, first, last):
+        at = slice(first - O + 8, last - O + 8)
+        value = (-0.5 * coef[r, at, :] * scale[r, at, :]) * yb[r, first:last, :]
+        ya[r, first:last, :] = value
+        return value * scale[r, at, :]
+
+    def start_inner(r, _):
+        keep(0, r - H, start_row(r, O, O + B))
+        return 0
+
+    groups(yb)
+    lax.fori_loop(6, RE - 6, start_inner, 0, unroll=7)
+    step_inside(ya, yb, 1, True, 2)
+    step_inside(yb, ya, 2, True, 2)
+    step_inside(ya, yb, 3, True, 2)
+    step_inside(yb, ya, 4, True, 2)
+
+    for copy in mask_copies:
+        copy.wait()
+    north_ok = (lat > 0).astype(F32)
+    south_ok = (lat < n_lat - 1).astype(F32)
+    low_lanes = lane_e[0:8] < 64
+    sm[0, 8:16, :] = mrx[2] * north_ok
+    sm[0, 16 + B : 24 + B, :] = mrx[3] * south_ok
+    sm[1, 8:16, :] = jnp.where(low_lanes, mrx[5], mrx[4]) * north_ok
+    sm[1, 16 : 16 + B, :] = jnp.concatenate(
+        [mrx[1], jnp.zeros((B - 16, B), F32), mrx[0]], axis=0
+    ).T
+    sm[1, 16 + B : 24 + B, :] = jnp.where(low_lanes, mrx[7], mrx[6]) * south_ok
+    degrees()
+    for p in (0, 1, 2, 17, 18, 19):
+        spread(p, 0)
+    lax.fori_loop(3, RE // 2 - 3, spread_sides, 0, unroll=7)
 
     for copy in first_halo:
         copy.wait()
-    groups(yb)
     assemble(0, yb, 1.0, 1.0)
-
-    def start_row(r, _):
-        x = yb[r, O - 8 : O + B + 8, :]
-        value = (-0.5 * coef[r] * scale[r]) * x
-        ya[r, O - 8 : O + B + 8, :] = value
-        return value
-
-    def start_halo(r, _):
-        start_row(r, 0)
-        return 0
-
-    def start_own(r, _):
-        keep(0, r - H, start_row(r, 0)[8 : 8 + B] * scale[r, 8 : 8 + B, :])
-        return 0
-
-    lax.fori_loop(0, H, start_halo, 0, unroll=4)
-    lax.fori_loop(H, H + R, start_own, 0, unroll=4)
-    lax.fori_loop(H + R, RE, start_halo, 0, unroll=4)
-
-    step(ya, yb, 1, True)
-    step(yb, ya, 2, True)
-    step(ya, yb, 3, True)
-    step(yb, ya, 4, True)
+    for r in tuple(range(6)) + tuple(range(RE - 6, RE)):
+        value = start_row(r, O - 8, O + B + 8)
+        if H <= r < H + R:
+            keep(0, r - H, value[8 : 8 + B])
+
+    def start_sides(r, _):
+        left = start_row(r, O - 8, O + 8)
+        right = start_row(r, O + B - 8, O + B + 8)
+        at = pl.multiple_of((r - H) * B, B)
+        terms[pl.ds(at, 8), 0:B] = left[8:16].astype(BF16)
+        terms[pl.ds(at + B - 8, 8), 0:B] = right[0:8].astype(BF16)
+        return 0
+
+    lax.fori_loop(6, RE - 6, start_sides, 0, unroll=7)
+    step_rim(ya, yb, 1, True, 2)
+    step_rim(yb, ya, 2, True, 2)
+    step_rim(ya, yb, 3, True, 2)
+    step_rim(yb, ya, 4, True, 2)
 
 
     def mix(p):
@@ -516,15 +498,15 @@
 
     lax.fori_loop(0, R, keep_grad, 0, unroll=4)
     groups(ya)
-    step_inside(ya, yb, 1)
-    step_inside(yb, ya, 2)
-    step_inside(ya, yb, 3)
-    step_inside(yb, ya, 4)
+    step_inside(ya, yb, 1, False, 0)
+    step_inside(yb, ya, 2, False, 0)
+    step_inside(ya, yb, 3, False, 0)
+    step_inside(yb, ya, 4, False, 0)
     for copy in second_halo:
         copy.wait()
     assemble(1, ya, north_ok, south_ok)
 
-    step_rim(ya, yb, 1)
+    step_rim(ya, yb, 1, False, 0)
 
     run(n_lon, lambda off: lon_wait(off).wait())
     total = ar1[0]
@@ -534,9 +516,9 @@
     run(n_lat, lambda off: lat_copy(off).start())
     ar2[lat] = total
 
-    step_rim(yb, ya, 2)
-    step_rim(ya, yb, 3)
-    step_rim(yb, ya, 4)
+    step_rim(yb, ya, 2, False, 0)
+    step_rim(ya, yb, 3, False, 0)
+    step_rim(yb, ya, 4, False, 0)
 
     def finish(p, _):
         t = terms[pl.ds(pl.multiple_of(2 * p * B, 2 * B), 2 * B), :]

time: 39.4 us -> 37.8 us (0.959)
  Pallas kernels: 38.7 us -> 37 us
    pallas_call x1, Pallas kernels: 37 us -> 35.4 us  [local(): pl.pallas_call(functools.partial(kernel, n_lat, n_lon), out_shape=carried...]
where the time goes in v8:
time: 37.8 us; the launch traced here: 37.6 us
  Pallas kernels  37 us (98%)
  between operations  0.64 us (2%)
    pallas_call x1, Pallas kernels, local(): pl.pallas_call(functools.partial(kernel, n_lat, n_lon), out_shape=carried...  35.4 us
    pallas_call x1, Pallas kernels, local(): pl.pallas_call(close, out_shape=(jax.ShapeDtypeStruct((C, B, B), BF16), j...  1.61 us

profile of v8, /device:TPU:1, one launch (start us, length us, event | category | flops | bytes accessed | tf_op | source)
XLA Modules:
  0.0 37.6 jit_solution(17781703580739927219)
XLA Ops:
  0.6 35.4 %shard_map.59 = (bf16[32,128,128]{2,1,0:T(8,128)(2,1)S(1)}, f32[40,128]{1,0:T(8,128)S(1)}) custom-call(bf16[32,128,128]{2,1,0:T(8,128)(2,1)} %feat_hbm.1, bf16[32,128,128]{2,1,0:T(8,128)(2,1)} %cot_hbm.1, s32[128,128]{1,0:T(8,128)} %mask_hbm.1, bf16[5,32,32]{2,1,0:T(8,128)(2,1)} %w_hbm.1), custom_call_target="tpu_custom_call" | custom-call | tf_op jit(solution)/shard_map/pallas_call | solution.py:572
  36.0 1.6 %shard_map.60 = (bf16[32,128,128]{2,1,0:T(8,128)(2,1)}, f32[5,32,32]{2,1,0:T(8,128)}) custom-call(bf16[32,128,128]{2,1,0:T(8,128)(2,1)S(1)} %get-tuple-element.4.out_v, f32[40,128]{1,0:T(8,128)S(1)} %get-tuple-element.5.sum_ref), custom_call_target="tpu_custom_call" | custom-call | tf_op jit(solution)/shard_map/pallas_call | solution.py:612

commit v9 on v8

--- a/solution.py
+++ b/solution.py
@@ -39,12 +39,19 @@
     north, south = lax.rem(lat + n_lat - 1, n_lat), lax.rem(lat + 1, n_lat)
     west, east = lax.rem(lon + n_lon - 1, n_lon), lax.rem(lon + 1, n_lon)
 
-    feat_in = pltpu.make_async_copy(feat_hbm, feat_v, in_sem.at[0])
+    part = C // 4
+    feat_in = [
+        pltpu.make_async_copy(
+            feat_hbm.at[pl.ds(n * part, part)], feat_v.at[pl.ds(n * part, part)], in_sem.at[4 + n]
+        )
+        for n in range(4)
+    ]
     cot_in = pltpu.make_async_copy(cot_hbm, cot_v, in_sem.at[1])
     mask_in = pltpu.make_async_copy(mask_hbm, mask_v, in_sem.at[2])
     w_in = pltpu.make_async_copy(w_hbm, w_v, in_sem.at[3])
     mask_in.start()
-    feat_in.start()
+    for copy in feat_in:
+        copy.start()
     w_in.start()
     cot_in.start()
 
@@ -167,21 +174,22 @@
             for copy in copies[10 + 2 * n : 12 + 2 * n]:
                 copy.start()
 
-    feat_in.wait()
-
-    def widen(src, dst):
+
+    def widen(src, dst, first, last):
         def body(c, _):
             dst[pl.ds(pl.multiple_of(c * B, B), B), :] = src[c].astype(F32)
             return 0
 
-        lax.fori_loop(0, C, body, 0, unroll=4)
+        lax.fori_loop(first, last, body, 0, unroll=4)
 
     def rows_of(flat, r):
         return jnp.concatenate(
             [flat[pl.ds(R * g + r, C, stride=B), :] for g in range(RG)], axis=0
         )
 
-    widen(feat_v, xf)
+    for n in range(4):
+        feat_in[n].wait()
+        widen(feat_v, xf, n * part, (n + 1) * part)
 
     def turn(r):
         yb[H + r, O : O + B, :] = rows_of(xf, r).T
@@ -203,7 +211,7 @@
         wf[:, k * B : (k + 1) * B] = full.T.astype(BF16)
 
     cot_in.wait()
-    widen(cot_v, cf)
+    widen(cot_v, cf, 0, C)
 
     lane_e = lax.broadcasted_iota(jnp.int32, (CE, B), 1)
     sm[...] = jnp.zeros_like(sm)
@@ -544,8 +552,15 @@
 
 
 def close(out_v, sum_ref, out_hbm, wg_ref, out_sem):
-    copy = pltpu.make_async_copy(out_v, out_hbm, out_sem)
-    copy.start()
+    part = C // 4
+    copies = [
+        pltpu.make_async_copy(
+            out_v.at[pl.ds(n * part, part)], out_hbm.at[pl.ds(n * part, part)], out_sem.at[n]
+        )
+        for n in range(4)
+    ]
+    for copy in copies:
+        copy.start()
     total = sum_ref[...]
     flat = total[0:C].T
     for k in range(K):
@@ -555,7 +570,8 @@
         [last if g == 0 else pltpu.roll(last, B - C * g, 1) for g in range(RG)], axis=0
     )
     wg_ref[K] = last.T[0:C, :]
-    copy.wait()
+    for copy in copies:
+        copy.wait()
 
 
 def solution(mesh):
@@ -602,7 +618,7 @@
                 pltpu.VMEM((2, C + 8, B), F32),
                 pltpu.VMEM((n_lon, C + 8, B), F32),
                 pltpu.VMEM((n_lat, C + 8, B), F32),
-                sem((4,)), sem((8,)), sem((8,)), sem((2, 16)), sem((2, 16)),
+                sem((8,)), sem((8,)), sem((8,)), sem((2, 16)), sem((2, 16)),
                 sem((n_lon,)), sem((n_lon,)), sem((n_lat,)), sem((n_lat,)),
             ],
             compiler_params=pltpu.CompilerParams(
@@ -617,7 +633,7 @@
             ),
             in_specs=[vmem] * 2,
             out_specs=(hbm, vmem),
-            scratch_shapes=[sem(())],
+            scratch_shapes=[sem((4,))],
             compiler_params=pltpu.CompilerParams(vmem_limit_bytes=4 << 20),
         )(*carried)
 

time: 37.8 us -> 37.8 us (level)
  no operation moved by 1% of the time
where the time goes in v9:
time: 37.8 us; the launch traced here: 37.7 us
  Pallas kernels  37.1 us (98%)
  between operations  0.64 us (2%)
    pallas_call x1, Pallas kernels, local(): pl.pallas_call(functools.partial(kernel, n_lat, n_lon), out_shape=carried...  35.4 us
    pallas_call x1, Pallas kernels, local(): pl.pallas_call(close, out_shape=(jax.ShapeDtypeStruct((C, B, B), BF16), j...  1.63 us

profile of v9, /device:TPU:1, one launch (start us, length us, event | category | flops | bytes accessed | tf_op | source)
XLA Modules:
  0.0 37.7 jit_solution(8541790665065697854)
XLA Ops:
  0.6 35.4 %shard_map.59 = (bf16[32,128,128]{2,1,0:T(8,128)(2,1)S(1)}, f32[40,128]{1,0:T(8,128)S(1)}) custom-call(bf16[32,128,128]{2,1,0:T(8,128)(2,1)} %feat_hbm.1, bf16[32,128,128]{2,1,0:T(8,128)(2,1)} %cot_hbm.1, s32[128,128]{1,0:T(8,128)} %mask_hbm.1, bf16[5,32,32]{2,1,0:T(8,128)(2,1)} %w_hbm.1), custom_call_target="tpu_custom_call" | custom-call | tf_op jit(solution)/shard_map/pallas_call | solution.py:588
  36.1 1.6 %shard_map.60 = (bf16[32,128,128]{2,1,0:T(8,128)(2,1)}, f32[5,32,32]{2,1,0:T(8,128)}) custom-call(bf16[32,128,128]{2,1,0:T(8,128)(2,1)S(1)} %get-tuple-element.4.out_v, f32[40,128]{1,0:T(8,128)S(1)} %get-tuple-element.5.sum_ref), custom_call_target="tpu_custom_call" | custom-call | tf_op jit(solution)/shard_map/pallas_call | solution.py:628

commit v10 on v8

--- a/solution.py
+++ b/solution.py
@@ -86,7 +86,6 @@
     mtx[1] = flags[:8]
     mtx[2] = turned_flags[B - 8 :]
     mtx[3] = turned_flags[:8]
-    pl.semaphore_wait(barrier, 4 + (n_lon - 1) + (n_lat - 1))
 
     def remote(src, dst, send, recv, i, j):
         return pltpu.make_async_remote_copy(
@@ -110,8 +109,6 @@
         remote(mtx.at[src], mrx.at[n], mask_send.at[n], mask_recv.at[n], i, j)
         for src, n, i, j in mask_plan
     ]
-    for copy in mask_copies:
-        copy.start()
 
     lane = lax.broadcasted_iota(jnp.int32, (B, B), 1)
 
@@ -190,8 +187,16 @@
         for r in range(first, first + count):
             turn(r)
 
+    turn_rows(0, R)
+    for p in range(R // 2):
+        pack_columns(0, yb, p)
+    pack_rows(0, yb)
+    pl.semaphore_wait(barrier, 4 + (n_lon - 1) + (n_lat - 1))
+    for copy in mask_copies:
+        copy.start()
     first_halo = halo_copies(0)
-    send_chunks(0, yb, first_halo, turn_rows)
+    for copy in first_halo:
+        copy.start()
 
     w_in.wait()
     block = (row_i // C) == (col_i // C)

time: 37.8 us -> 36.7 us (0.971)
  Pallas kernels: 37 us -> 35.9 us
    pallas_call x1, Pallas kernels: 35.4 us -> 34.3 us  [local(): pl.pallas_call(functools.partial(kernel, n_lat, n_lon), out_shape=carried...]
where the time goes in v10:
time: 36.7 us; the launch traced here: 36.5 us
  Pallas kernels  35.9 us (98%)
  between operations  0.64 us (2%)
    pallas_call x1, Pallas kernels, local(): pl.pallas_call(functools.partial(kernel, n_lat, n_lon), out_shape=carried...  34.3 us
    pallas_call x1, Pallas kernels, local(): pl.pallas_call(close, out_shape=(jax.ShapeDtypeStruct((C, B, B), BF16), j...  1.61 us

profile of v10, /device:TPU:1, one launch (start us, length us, event | category | flops | bytes accessed | tf_op | source)
XLA Modules:
  0.0 36.5 jit_solution(17848148530922553607)
XLA Ops:
  0.6 34.3 %shard_map.59 = (bf16[32,128,128]{2,1,0:T(8,128)(2,1)S(1)}, f32[40,128]{1,0:T(8,128)S(1)}) custom-call(bf16[32,128,128]{2,1,0:T(8,128)(2,1)} %feat_hbm.1, bf16[32,128,128]{2,1,0:T(8,128)(2,1)} %cot_hbm.1, s32[128,128]{1,0:T(8,128)} %mask_hbm.1, bf16[5,32,32]{2,1,0:T(8,128)(2,1)} %w_hbm.1), custom_call_target="tpu_custom_call" | custom-call | tf_op jit(solution)/shard_map/pallas_call | solution.py:577
  34.9 1.6 %shard_map.60 = (bf16[32,128,128]{2,1,0:T(8,128)(2,1)}, f32[5,32,32]{2,1,0:T(8,128)}) custom-call(bf16[32,128,128]{2,1,0:T(8,128)(2,1)S(1)} %get-tuple-element.4.out_v, f32[40,128]{1,0:T(8,128)S(1)} %get-tuple-element.5.sum_ref), custom_call_target="tpu_custom_call" | custom-call | tf_op jit(solution)/shard_map/pallas_call | solution.py:617

commit v11 on v8

--- a/solution.py
+++ b/solution.py
@@ -86,7 +86,6 @@
     mtx[1] = flags[:8]
     mtx[2] = turned_flags[B - 8 :]
     mtx[3] = turned_flags[:8]
-    pl.semaphore_wait(barrier, 4 + (n_lon - 1) + (n_lat - 1))
 
     def remote(src, dst, send, recv, i, j):
         return pltpu.make_async_remote_copy(
@@ -110,8 +109,6 @@
         remote(mtx.at[src], mrx.at[n], mask_send.at[n], mask_recv.at[n], i, j)
         for src, n, i, j in mask_plan
     ]
-    for copy in mask_copies:
-        copy.start()
 
     lane = lax.broadcasted_iota(jnp.int32, (B, B), 1)
 
@@ -190,9 +187,6 @@
         for r in range(first, first + count):
             turn(r)
 
-    first_halo = halo_copies(0)
-    send_chunks(0, yb, first_halo, turn_rows)
-
     w_in.wait()
     block = (row_i // C) == (col_i // C)
     for k in range(K + 1):
@@ -201,6 +195,17 @@
         full = jnp.where(block, jnp.concatenate([wide] * RG, axis=0), 0.0)
         wb[:, k * B : (k + 1) * B] = full.astype(BF16)
         wf[:, k * B : (k + 1) * B] = full.T.astype(BF16)
+
+    turn_rows(0, R)
+    for p in range(R // 2):
+        pack_columns(0, yb, p)
+    pack_rows(0, yb)
+    pl.semaphore_wait(barrier, 4 + (n_lon - 1) + (n_lat - 1))
+    for copy in mask_copies:
+        copy.start()
+    first_halo = halo_copies(0)
+    for copy in first_halo:
+        copy.start()
 
     cot_in.wait()
     widen(cot_v, cf)

time: 37.8 us -> 36.7 us (0.971)
  Pallas kernels: 37 us -> 36 us
    pallas_call x1, Pallas kernels: 35.4 us -> 34.4 us  [local(): pl.pallas_call(functools.partial(kernel, n_lat, n_lon), out_shape=carried...]
where the time goes in v11:
time: 36.7 us; the launch traced here: 36.6 us
  Pallas kernels  36 us (98%)
  between operations  0.64 us (2%)
    pallas_call x1, Pallas kernels, local(): pl.pallas_call(functools.partial(kernel, n_lat, n_lon), out_shape=carried...  34.4 us
    pallas_call x1, Pallas kernels, local(): pl.pallas_call(close, out_shape=(jax.ShapeDtypeStruct((C, B, B), BF16), j...  1.61 us

profile of v11, /device:TPU:1, one launch (start us, length us, event | category | flops | bytes accessed | tf_op | source)
XLA Modules:
  0.0 36.6 jit_solution(10811836581411494087)
XLA Ops:
  0.6 34.4 %shard_map.59 = (bf16[32,128,128]{2,1,0:T(8,128)(2,1)S(1)}, f32[40,128]{1,0:T(8,128)S(1)}) custom-call(bf16[32,128,128]{2,1,0:T(8,128)(2,1)} %feat_hbm.1, bf16[32,128,128]{2,1,0:T(8,128)(2,1)} %cot_hbm.1, s32[128,128]{1,0:T(8,128)} %mask_hbm.1, bf16[5,32,32]{2,1,0:T(8,128)(2,1)} %w_hbm.1), custom_call_target="tpu_custom_call" | custom-call | tf_op jit(solution)/shard_map/pallas_call | solution.py:577
  35.0 1.6 %shard_map.60 = (bf16[32,128,128]{2,1,0:T(8,128)(2,1)}, f32[5,32,32]{2,1,0:T(8,128)}) custom-call(bf16[32,128,128]{2,1,0:T(8,128)(2,1)S(1)} %get-tuple-element.4.out_v, f32[40,128]{1,0:T(8,128)S(1)} %get-tuple-element.5.sum_ref), custom_call_target="tpu_custom_call" | custom-call | tf_op jit(solution)/shard_map/pallas_call | solution.py:617
